TPU v7x, 256 devices: a whole 4x4x8 slice. The times are simulated.
256 devices in a mesh: grp: 16 (over z, core), leaf: 16 (over y, x).
Axes of the slice: x: 4, y: 4, z: 8, core: 2. Of those that a mesh axis runs over, the one named last changes fastest.
Arguments:
- near_tiles: float32 [512, 16, 256, 256], P(('grp', 'leaf')), may hold values from -0.15625 to 0.15625
- diag_tiles: float32 [512, 256, 256], P(('grp', 'leaf')), as said below
- near_index: int32 [512, 16], P(('grp', 'leaf')), may hold values from 0 to 511, as said below
- near_mask: int32 [512, 16], P(('grp', 'leaf')), may hold values from 0 to 1
- leaf_basis: float32 [512, 256, 256], P(('grp', 'leaf')), as said below
- level1_basis: float32 [256, 256, 256], P(('grp', 'leaf')), as said below
- level2_basis: float32 [32768, 256], P(('grp', 'leaf')), as said below
Outputs:
- leaf_factor: float32 [512, 128, 128], P(('grp', 'leaf'))
- level1_factor: float32 [256, 128, 128], P(('grp', 'leaf'))
- level2_factor: float32 [16384, 128], P(('grp', 'leaf'))
- top_schur: float32 [16384, 128], P(('grp', 'leaf'))
- top_coupling: float32 [16384, 512], P(('grp', 'leaf'))
- log_det: float32 [], replicated
Inputs may be any that keep to these rules, and one draw needn't show every extreme that they name: `near_index`: slot t of row i names box i + o for distinct nonzero offsets o with |o| <= 8, clipped to the range of boxes; a live slot is never clipped. `diag_tiles`: each tile is symmetric and positive definite. `leaf_basis`: each tile is orthogonal. `level1_basis`: each tile is orthogonal. `level2_basis`: each group's 2 * 128 rows form an orthogonal matrix.
All inputs are finite; a program needn't handle non-finite values.
Results may differ from a plain program's by a relative error of at most 0.0003.
Values sent between devices are 32-bit elements; how exact they have to be, the bound alone decides.
A program may use at most 128 MiB of HBM per device.

v0:
```python
import jax
import jax.numpy as jnp
from jax import lax
from jax.sharding import Mesh
from jax.sharding import PartitionSpec as P

LEAF = 256
RANK = 128
NEAR = 16
GRP_LEAF = ("grp_0", "grp_1", "leaf_0", "leaf_1")
LEAF_AXES = ("leaf_0", "leaf_1")


highest = lax.Precision.HIGHEST


def shifted(block, axis, distance):
    devices = range(lax.axis_size(axis))
    route = [((i - distance) % len(devices), i) for i in devices]
    return lax.ppermute(block, axis, route)


def from_partner(value, axis, stride):
    mask = 2**stride
    pairs = [(source, source ^ mask) for source in range(lax.axis_size(axis))]
    return lax.ppermute(value, axis, pairs)


def by_axis(value, axes):
    for axis in axes:
        value = lax.psum(value, axis)
    return value


def product(left, right):
    return jnp.matmul(left, right, precision=highest)


def factor_box(diagonal, transform, skeleton):
    redundant = diagonal.shape[0] - skeleton
    symmetric = 0.5 * (diagonal + diagonal.T)
    turned = product(product(transform.T, symmetric), transform)
    factor = jnp.linalg.cholesky(turned[:redundant, :redundant])
    panel_block = jax.scipy.linalg.solve_triangular(
        factor, turned[:redundant, redundant:], lower=True
    )
    schur_block = turned[redundant:, redundant:] - product(panel_block.T, panel_block)
    return (factor, panel_block, schur_block)


def couple(near_block, transform, panel_block, factor, target):
    redundant = factor.shape[0]
    rotated = product(transform.T, product(near_block, target))
    carried = jax.scipy.linalg.solve_triangular(factor, rotated[:redundant], lower=True)
    return rotated[redundant:] - product(panel_block.T, carried)


def couple_slots(near_blocks, transform, panel_block, factor, targets):
    return jax.vmap(couple, in_axes=(0, None, None, None, 0))(
        near_blocks, transform, panel_block, factor, targets
    )


def assemble_parents(coupling, schur_block, near_ids, live_mask, leaf_ids, radius):
    number = coupling.shape[0]
    skeleton = coupling.shape[2]
    parent = leaf_ids // 2
    offset = near_ids // 2 - parent[:, None] + radius
    choose_box = (
        offset[:, :, None] == jnp.arange(2 * radius + 1, dtype=jnp.int32)[None, None, :]
    ).astype(jnp.float32)
    choose_box = choose_box * live_mask.astype(jnp.float32)[:, :, None]
    choose_half = (
        (near_ids % 2)[:, :, None] == jnp.arange(2, dtype=jnp.int32)[None, None, :]
    ).astype(jnp.float32)
    weights = choose_box[:, :, :, None] * choose_half[:, :, None, :]
    blocks = jnp.einsum("nsdb,nsij->ndbij", weights, coupling, precision=highest)
    own_half = ((leaf_ids % 2)[:, None] == jnp.arange(2, dtype=jnp.int32)[None, :]).astype(
        jnp.float32
    )
    blocks = blocks.at[:, radius].add(own_half[:, :, None, None] * schur_block[:, None])
    blocks = blocks.reshape(number // 2, 2, 2 * radius + 1, 2, skeleton, skeleton).transpose(
        0, 2, 1, 4, 3, 5
    )
    return blocks.reshape(number // 2, 2 * radius + 1, 2 * skeleton, 2 * skeleton)


def level_couplings(blocks, transform, panel_block, factor, window, position, radius):
    offsets = [offset_slot for offset_slot in range(2 * radius + 1) if offset_slot != radius]
    targets = jnp.take(window, position + jnp.array(offsets, dtype=jnp.int32), axis=0)
    chosen = jnp.stack([blocks[offset_slot] for offset_slot in offsets])
    return couple_slots(chosen, transform, panel_block, factor, targets)


def assemble_top(coupling, schur_block):
    filler = jnp.zeros_like(schur_block[0])
    leaf_offsets = [-4, -3, -2, -1, 1, 2, 3, 4]
    slot_list = []
    for level_step in range(-2, 3):
        row_list = []
        for child_row in range(2):
            col_list = []
            for child_col in range(2):
                distance = 2 * level_step + child_col - child_row
                if distance == 0:
                    col_list.append(schur_block[child_row])
                elif distance in leaf_offsets:
                    col_list.append(coupling[child_row, leaf_offsets.index(distance)])
                else:
                    col_list.append(filler)
            row_list.append(jnp.concatenate(col_list, axis=1))
        slot_list.append(jnp.concatenate(row_list, axis=0))
    return jnp.stack(slot_list)


def log_sum(factor):
    return jnp.sum(jnp.log(jnp.diagonal(factor, axis1=-2, axis2=-1)))


def neighbours(skeleton_bases):
    inner = []
    for distance in (-1, 0, 1):
        if distance == 0:
            inner.append(skeleton_bases)
        else:
            inner.append(shifted(skeleton_bases, GRP_LEAF, -distance))
    middle = jnp.concatenate(inner, axis=0)
    outer = []
    for stride in (3, -3):
        outer.append(shifted(middle, GRP_LEAF, stride))
    return jnp.concatenate([outer[0], middle, outer[1]], axis=0)


def on_device(
    near_tiles, diag_tiles, near_index, near_mask, leaf_basis, level1_basis, level2_basis
):
    device = lax.axis_index(GRP_LEAF)
    even_side = lax.axis_index(LEAF_AXES) % 2 == 0
    leaf_count = diag_tiles.shape[0]
    leaf_ids = leaf_count * device + jnp.arange(leaf_count, dtype=jnp.int32)
    leaf_lower, leaf_panel, leaf_schur = jax.vmap(factor_box, in_axes=(0, 0, None))(
        diag_tiles, leaf_basis, RANK
    )
    leaf_window = neighbours(leaf_basis[:, :, LEAF - RANK :])
    window_ids = near_index - leaf_count * (device - 4)
    targets = jnp.take(leaf_window, window_ids.reshape(-1), axis=0).reshape(
        leaf_count, NEAR, LEAF, RANK
    )
    coupling = jax.vmap(couple_slots)(near_tiles, leaf_basis, leaf_panel, leaf_lower, targets)
    coupling = coupling * near_mask.astype(jnp.float32)[:, :, None, None]
    blocks = assemble_parents(coupling, leaf_schur, near_index, near_mask, leaf_ids, 4)[0]
    parent_basis = level1_basis[0]
    parent_lower, parent_panel, parent_schur = factor_box(blocks[4], parent_basis, RANK)
    parent_window = neighbours(level1_basis[:, :, RANK:])
    parent_coupling = level_couplings(
        blocks, parent_basis, parent_panel, parent_lower, parent_window, 0, 4
    )
    partner = from_partner((parent_schur, parent_coupling, level2_basis), LEAF_AXES, 0)
    schur_pair = jnp.stack(
        [
            jnp.where(even_side, parent_schur, partner[0]),
            jnp.where(even_side, partner[0], parent_schur),
        ]
    )
    coupling_pair = jnp.stack(
        [
            jnp.where(even_side, parent_coupling, partner[1]),
            jnp.where(even_side, partner[1], parent_coupling),
        ]
    )
    group_basis = jnp.where(
        even_side,
        jnp.concatenate([level2_basis, partner[2]], axis=0),
        jnp.concatenate([partner[2], level2_basis], axis=0),
    )
    group_blocks = assemble_top(coupling_pair, schur_pair)
    top_lower, top_panel, top_schur = factor_box(group_blocks[2], group_basis, RANK)
    group_skeleton = group_basis[:, RANK:]
    pieces = []
    for distance in range(-2, 3):
        if distance == 0:
            pieces.append(group_skeleton)
        else:
            pieces.append(shifted(group_skeleton, GRP_LEAF, -2 * distance))
    group_window = jnp.stack(pieces)
    top_coupling = level_couplings(
        group_blocks, group_basis, top_panel, top_lower, group_window, 0, 2
    )
    own_terms = 2.0 * (log_sum(leaf_lower) + log_sum(parent_lower))
    own_terms = own_terms + jnp.where(even_side, 2.0 * log_sum(top_lower), jnp.float32(0.0))
    log_det = by_axis(own_terms, GRP_LEAF)
    half_rows = RANK // 2
    row_start = jnp.where(even_side, 0, half_rows).astype(jnp.int32)
    level2_factor = lax.dynamic_slice_in_dim(top_lower, row_start, half_rows, 0)
    schur_rows = lax.dynamic_slice_in_dim(top_schur, row_start, half_rows, 0)
    side_by_side = top_coupling.transpose(1, 0, 2).reshape(RANK, 4 * RANK)
    coupling_rows = lax.dynamic_slice_in_dim(side_by_side, row_start, half_rows, 0)
    return (leaf_lower, parent_lower[None], level2_factor, schur_rows, coupling_rows, log_det)


def solution(mesh):
    torus = Mesh(mesh.devices.reshape(8, 2, 4, 4), ("grp_0", "grp_1", "leaf_0", "leaf_1"))
    in_specs = (
        P(GRP_LEAF, None, None, None),
        P(GRP_LEAF, None, None),
        P(GRP_LEAF, None),
        P(GRP_LEAF, None),
        P(GRP_LEAF, None, None),
        P(GRP_LEAF, None, None),
        P(GRP_LEAF, None),
    )
    out_specs = (
        P(GRP_LEAF, None, None),
        P(GRP_LEAF, None, None),
        P(GRP_LEAF, None),
        P(GRP_LEAF, None),
        P(GRP_LEAF, None),
        P(),
    )
    return jax.shard_map(
        on_device, mesh=torus, in_specs=in_specs, out_specs=out_specs, check_vma=False
    )
```

profile of v0, /device:TPU:2, one launch (start us, length us, event | category | flops | bytes accessed | tf_op | source)
XLA Modules:
  0.0 305.6 jit_solution(775952343479033070)
XLA Ops:
  0.7 1.1 slice.224
  1.7 2.3 collective-permute-start.1
  4.0 1.6 slice.249
  5.6 8.2 %collective-permute-start.7 = (f32[1,256,128]{2,1,0:T(8,128)}, f32[1,256,128]{2,1,0:T(8,128)S(1)}, u32[]{:S(2)}, u32[]{:S(2)}) collective-permute-start(f32[1,256,128]{2,1,0:T(8,128)} %slice.249), channel_id=1, source_target_pairs={{1,0},{2,1},{3,2},{4,3},{5,4},{6,5},{7,6},{8,7},{9,8},{10,9},{11,1... | collective-permute-start | bytes 393224 | tf_op jit(solution)/shard_map/ppermute | solution.py:20
  13.8 7.3 %collective-permute-start.4 = (f32[128,256]{1,0:T(8,128)}, f32[128,256]{1,0:T(8,128)}, u32[]{:S(2)}, u32[]{:S(2)}) collective-permute-start(f32[128,256]{1,0:T(8,128)} %param.20), channel_id=1, source_target_pairs={{0,1},{1,0},{2,3},{3,2},{4,5},{5,4},{6,7},{7,6},{8,9},{9,8},{10,11... | collective-permute-start | bytes 393224 | tf_op jit(solution)/shard_map/ppermute | solution.py:26
  21.2 1.2 copy.59
  22.5 1.1 fusion.29
  23.6 0.7 fusion.82
  24.4 23.5 %custom-call.24 = f32[2,128,128]{2,1,0:T(8,128)S(1)} custom-call(f32[2,128,128]{2,1,0:T(8,128)S(1)} %fusion.53), custom_call_target="Cholesky" | custom-call | tf_op jit(solution)/shard_map/vmap(jit(cholesky))/cholesky | solution.py:43
  48.8 19.7 %custom-call.25 = f32[2,1,128,128]{2,3,1,0:T(8,128)S(1)} custom-call(f32[2,1,128,128]{3,2,1,0:T(8,128)S(1)} %get-tuple-element.24), custom_call_target="InvertDiagBlocksLowerTriangular" | custom-call | tf_op jit(solution)/shard_map/vmap(jit(_solve_triangular))/triangular_solve | solution.py:44
  69.0 1.0 convolution_subtract_fusion
  71.9 4.6 %copy.110 = f32[2,128,128]{0,2,1:T(8,128)} copy(f32[2,128,128]{2,1,0:T(8,128)S(1)} %get-tuple-element.25) | data formatting | bytes 262144 | tf_op jit(solution)/shard_map/vmap(jit(cholesky))/select_n | solution.py:43
  76.5 1.8 gather_fusion.3
  78.3 0.7 log_reduce_fusion
  79.0 1.0 maximum_select_fusion
  80.2 1.8 pad_maximum_fusion.1
  82.0 6.5 %collective-permute-start.9 = (f32[3,256,128]{2,1,0:T(8,128)}, f32[3,256,128]{2,1,0:T(8,128)}, u32[]{:S(2)}, u32[]{:S(2)}) collective-permute-start(f32[3,256,128]{2,1,0:T(8,128)} %pad_maximum_fusion.1), channel_id=1, source_target_pairs={{3,0},{4,1},{5,2},{6,3},{7,4},{8,5},{9,6},{10,7},{11,8},{12,9},{13... | collective-permute-start | bytes 1179656 | tf_op jit(solution)/shard_map/ppermute | solution.py:20
  89.4 7.1 %collective-permute-start.13 = (f32[256,128]{1,0:T(8,128)S(1)}, f32[256,128]{1,0:T(8,128)S(1)}, u32[]{:S(2)}, u32[]{:S(2)}) collective-permute-start(f32[256,128]{1,0:T(8,128)S(1)} %slice.324), channel_id=1, source_target_pairs={{2,0},{3,1},{4,2},{5,3},{6,4},{7,5},{8,6},{9,7},{10,8},{11,9},{12,... | collective-permute-start | bytes 393224 | tf_op jit(solution)/shard_map/ppermute | solution.py:20
  96.5 1.0 pad_maximum_fusion
  97.5 1.6 collective-permute-done.12
  99.1 2.6 collective-permute-start.2
  101.7 6.4 %collective-permute-start.3 = (f32[6,256,128]{2,1,0:T(8,128)}, f32[6,256,128]{2,1,0:T(8,128)}, u32[]{:S(2)}, u32[]{:S(2)}) collective-permute-start(f32[6,256,128]{2,1,0:T(8,128)} %pad_maximum_fusion), channel_id=1, source_target_pairs={{3,0},{4,1},{5,2},{6,3},{7,4},{8,5},{9,6},{10,7},{11,8},{12,9},{13... | collective-permute-start | bytes 2359304 | tf_op jit(solution)/shard_map/ppermute | solution.py:20
  108.2 7.3 %collective-permute-done.14 = f32[256,128]{1,0:T(8,128)S(1)} collective-permute-done((f32[256,128]{1,0:T(8,128)S(1)}, f32[256,128]{1,0:T(8,128)S(1)}, u32[]{:S(2)}, u32[]{:S(2)}) %collective-permute-start.14) | collective-permute-done | bytes 131104 | tf_op jit(solution)/shard_map/ppermute | solution.py:20
  115.5 1.4 gather_fusion.2
  116.9 1.0 constant_dynamic-update-slice_fusion.9
  118.0 1.0 constant_dynamic-update-slice_fusion.5
  119.0 1.8 gather_fusion.1
  120.8 1.2 constant_dynamic-update-slice_fusion.4
  122.1 1.0 constant_dynamic-update-slice_fusion.3
  123.1 1.2 constant_dynamic-update-slice_fusion
  124.3 2.8 gather_fusion
  127.1 5.8 %copy.64 = f32[2,16,256,128]{2,3,1,0:T(8,128)} copy(f32[2,16,256,128]{3,2,1,0:T(8,128)} %bitcast.250) | data formatting | bytes 8388608 | tf_op jit(solution)/shard_map/jit(_take)/gather | solution.py:146
  132.9 13.4 %fusion.2 = f32[2,16,128,256]{3,2,1,0:T(8,128)S(1)} fusion(f32[2,16,256,256]{3,2,1,0:T(8,128)} %param.14, f32[2,16,256,128]{2,3,1,0:T(8,128)} %copy.64, pred[2,16]{1,0:T(4,128)(4,1)S(1)} %copy-done.22), kind=kOutput, calls=%fused_computation.8 | convolution fusion | flops 3222274048 | bytes 16777248 | tf_op jit(solution)/shard_map/vmap(vmap())/dot_general | solution.py:36
  146.3 4.1 %fusion.4 = f32[2,256,16,128]{1,3,2,0:T(8,128)S(1)} fusion(f32[2,16,128,256]{3,2,1,0:T(8,128)S(1)} %fusion.2, f32[2,256,256]{2,1,0:T(8,128)S(1)} %copy-done.1), kind=kOutput, calls=%fused_computation.10 | convolution fusion | flops 3221225472 | bytes 8912896 | tf_op jit(solution)/shard_map/vmap(vmap())/dot_general | solution.py:36
  150.6 1.4 copy.66
  152.0 1.8 fusion.50
  153.8 2.8 fusion.9
  156.6 2.0 copy.121
  158.6 5.0 %fusion.68 = f32[2,9,2,128,128]{4,1,3,2,0:T(8,128)S(1)} fusion(f32[2,16,128,128,1]{3,1,2,4,0:T(8,128)} %copy.121, f32[2,16,2]{1,2,0:T(2,128)S(1)} %compare_convert_fusion, f32[2,16,9]{1,2,0:T(8,128)S(1)} %copy-done.20), kind=kOutput, calls=%fused_computation.150 | convolution fusion | flops 113246784 | bytes 4457856 | tf_op jit(solution)/shard_map/nsdb,nsij->ndbij/dot_general | solution.py:77
  163.6 1.9 copy-done
  165.9 8.2 %scatter-add.4 = f32[1,2,9,2,128,128]{5,2,4,3,1,0:T(8,128)} dynamic-update-slice(f32[1,2,9,2,128,128]{5,2,4,3,1,0:T(8,128)} %bitcast.251, f32[1,2,1,2,128,128]{5,2,4,3,1,0:T(1,128)S(1)} %fusion.33, s32[]{:T(128)} %constant.247.clone.1, s32[]{:T(128)} %constant.247.clone.1, s32[]{:T(128)} %constant.251.clone.1, s32[]{:T(128)} %constant.247.clone.1, s32[]{:T(128)} %constant.247.clone.1, ...) | dynamic-update-slice | bytes 524292 | tf_op jit(solution)/shard_map/scatter-add | solution.py:81
  174.2 9.8 %fusion.80 = (f32[1,1,2,128,2,128]{5,1,3,4,2,0:T(1,128)S(1)}, f32[1,1,2,128,2,128]{5,1,3,4,2,0:T(1,128)S(1)}, f32[1,1,2,128,2,128]{5,1,3,4,2,0:T(1,128)S(1)}, f3...) fusion(f32[1,9,2,128,2,128]{5,1,3,4,2,0:T(8,128)} %bitcast.252), kind=kLoop, calls=%fused_computation.196 | loop fusion | bytes 4718592 | tf_op jit(solution)/shard_map/slice | solution.py:91
  184.2 0.8 copy.77
  185.0 1.3 fusion.40
  187.1 11.7 %cholesky.83 = f32[128,128]{1,0:T(8,128)S(1)} custom-call(f32[128,128]{1,0:T(8,128)S(1)} %fusion.67), custom_call_target="Cholesky" | custom-call | tf_op jit(solution)/shard_map/jit(cholesky)/cholesky | solution.py:43
  199.5 0.7 select_bitcast_fusion.4
  200.2 9.8 %custom-call.35 = f32[1,128,128]{1,2,0:T(8,128)S(1)} custom-call(f32[1,128,128]{2,1,0:T(8,128)S(1)} %get-tuple-element.22), custom_call_target="InvertDiagBlocksLowerTriangular" | custom-call | tf_op jit(solution)/shard_map/jit(_solve_triangular)/triangular_solve | solution.py:44
  212.2 0.8 copy-done.4
  213.0 2.5 fusion.83
  215.5 1.2 convolution_bitcast_fusion
  218.3 2.1 collective-permute-start.5
  220.4 1.2 gather_fusion.4
  223.6 7.8 %collective-permute-done.5 = f32[128,128]{0,1:T(8,128)S(1)} collective-permute-done((f32[128,128]{0,1:T(8,128)S(1)}, f32[128,128]{0,1:T(8,128)S(1)}, u32[]{:S(2)}, u32[]{:S(2)}) %collective-permute-start.5) | collective-permute-done | bytes 65568 | tf_op jit(solution)/shard_map/ppermute | solution.py:26
  231.5 0.7 slice_bitcast_fusion.17
  233.5 11.7 %cholesky.94 = f32[128,128]{1,0:T(8,128)S(1)} custom-call(f32[128,128]{1,0:T(8,128)S(1)} %get-tuple-element.56), custom_call_target="Cholesky" | custom-call | tf_op jit(solution)/shard_map/jit(cholesky)/cholesky | solution.py:43
  245.9 0.7 select_bitcast_fusion.3
  246.6 9.8 %custom-call.36 = f32[1,128,128]{1,2,0:T(8,128)S(1)} custom-call(f32[1,128,128]{2,1,0:T(8,128)S(1)} %get-tuple-element.20), custom_call_target="InvertDiagBlocksLowerTriangular" | custom-call | tf_op jit(solution)/shard_map/jit(_solve_triangular)/triangular_solve | solution.py:44
  256.5 1.1 fusion.18
  258.5 1.2 gather_fusion.5
  261.7 17.1 %psum.28 = f32[]{:T(128)} all-reduce(f32[]{:T(128)S(6)} %add.185), channel_id=1, replica_groups=mesh['grp_0'=8,'grp_1'=2,'leaf_0'=4,'leaf_1'=4] {'grp_0'}, use_global_device_ids=true, to_apply=%region_7.10 | all-reduce | flops 1 | bytes 8 | tf_op jit(solution)/shard_map/psum | solution.py:31
  279.5 3.1 %psum.29 = f32[]{:T(128)} all-reduce(f32[]{:T(128)} %psum.28), channel_id=1, replica_groups=mesh['grp_0'=8,'grp_1'=2,'leaf_0'=4,'leaf_1'=4] {'grp_1'}, use_global_device_ids=true, to_apply=%region_8.11 | all-reduce | flops 1 | bytes 8 | tf_op jit(solution)/shard_map/psum | solution.py:31
  283.3 10.8 %psum.30 = f32[]{:T(128)} all-reduce(f32[]{:T(128)} %psum.29), channel_id=1, replica_groups=mesh['grp_0'=8,'grp_1'=2,'leaf_0'=4,'leaf_1'=4] {'leaf_0'}, use_global_device_ids=true, to_apply=%region_9.12 | all-reduce | flops 1 | bytes 8 | tf_op jit(solution)/shard_map/psum | solution.py:31
  294.1 0.8 copy.139
  294.8 10.0 %psum.31 = f32[]{:T(128)} all-reduce(f32[]{:T(128)} %psum.30), channel_id=1, replica_groups=mesh['grp_0'=8,'grp_1'=2,'leaf_0'=4,'leaf_1'=4] {'leaf_1'}, use_global_device_ids=true, to_apply=%region_10.13 | all-reduce | flops 1 | bytes 8 | tf_op jit(solution)/shard_map/psum | solution.py:31
  (162 shorter events, 17.2 us)
Async XLA Ops:
  0.6 21.8 %copy-start.1 = (f32[2,256,256]{2,1,0:T(8,128)S(1)}, f32[2,256,256]{2,1,0:T(8,128)}, u32[]{:S(2)}) copy-start(f32[2,256,256]{2,1,0:T(8,128)} %param.18) | copy-start | bytes 1572868
  0.6 21.8 %copy-start.5 = (f32[2,256,256]{2,1,0:T(8,128)S(1)}, f32[2,256,256]{2,1,0:T(8,128)}, u32[]{:S(2)}) copy-start(f32[2,256,256]{2,1,0:T(8,128)} %param.15) | copy-start | bytes 1572868
  1.7 87.7 %collective-permute-start.1 = (f32[2,256,128]{2,1,0:T(8,128)S(1)}, f32[2,256,128]{2,1,0:T(8,128)S(1)}, u32[]{:S(2)}, u32[]{:S(2)}) collective-permute-start(f32[2,256,128]{2,1,0:T(8,128)S(1)} %slice.224), channel_id=1, source_target_pairs={{1,0},{2,1},{3,2},{4,3},{5,4},{6,5},{7,6},{8,7},{9,8},{10,9},{11,1... | collective-permute-start | bytes 786440 | tf_op jit(solution)/shard_map/ppermute | solution.py:20
  4.0 92.5 %collective-permute-start = (f32[2,256,128]{2,1,0:T(8,128)S(1)}, f32[2,256,128]{2,1,0:T(8,128)S(1)}, u32[]{:S(2)}, u32[]{:S(2)}) collective-permute-start(f32[2,256,128]{2,1,0:T(8,128)S(1)} %slice.224), channel_id=1, source_target_pairs={{255,0},{0,1},{1,2},{2,3},{3,4},{4,5},{5,6},{6,7},{7,8},{8,9},{9,1... | collective-permute-start | bytes 786440 | tf_op jit(solution)/shard_map/ppermute | solution.py:20
  5.6 74.5 %collective-permute-start.7 = (f32[1,256,128]{2,1,0:T(8,128)}, f32[1,256,128]{2,1,0:T(8,128)S(1)}, u32[]{:S(2)}, u32[]{:S(2)}) collective-permute-start(f32[1,256,128]{2,1,0:T(8,128)} %slice.249), channel_id=1, source_target_pairs={{1,0},{2,1},{3,2},{4,3},{5,4},{6,5},{7,6},{8,7},{9,8},{10,9},{11,1... | collective-permute-start | bytes 393224 | tf_op jit(solution)/shard_map/ppermute | solution.py:20
  13.8 66.3 %collective-permute-start.6 = (f32[1,256,128]{2,1,0:T(8,128)}, f32[1,256,128]{2,1,0:T(8,128)S(1)}, u32[]{:S(2)}, u32[]{:S(2)}) collective-permute-start(f32[1,256,128]{2,1,0:T(8,128)} %slice.249), channel_id=1, source_target_pairs={{255,0},{0,1},{1,2},{2,3},{3,4},{4,5},{5,6},{6,7},{7,8},{8,9},{9,1... | collective-permute-start | bytes 393224 | tf_op jit(solution)/shard_map/ppermute | solution.py:20
  13.8 65.1 %collective-permute-start.4 = (f32[128,256]{1,0:T(8,128)}, f32[128,256]{1,0:T(8,128)}, u32[]{:S(2)}, u32[]{:S(2)}) collective-permute-start(f32[128,256]{1,0:T(8,128)} %param.20), channel_id=1, source_target_pairs={{0,1},{1,0},{2,3},{3,2},{4,5},{5,4},{6,7},{7,6},{8,9},{9,8},{10,11... | collective-permute-start | bytes 393224 | tf_op jit(solution)/shard_map/ppermute | solution.py:26
  22.5 25.6 %copy-start.21 = (s32[2,16]{1,0:T(2,128)S(1)}, s32[2,16]{1,0:T(2,128)}, u32[]{:S(2)}) copy-start(s32[2,16]{1,0:T(2,128)} %param.16) | copy-start | bytes 388
  22.5 46.0 %copy-start.24 = (s32[2,16]{1,0:T(2,128)S(1)}, s32[2,16]{1,0:T(2,128)}, u32[]{:S(2)}) copy-start(s32[2,16]{1,0:T(2,128)} %param.17) | copy-start | bytes 388
  23.6 47.1 %copy-start.26 = (s32[8]{0:T(128)S(1)}, s32[8]{0:T(128)}, u32[]{:S(2)}) copy-start(s32[8]{0:T(128)} %constant.335) | copy-start | bytes 100
  48.7 27.7 %copy-start.10 = (f32[2,128,128]{2,1,0:T(8,128)}, f32[2,128,128]{2,1,0:T(8,128)S(1)}, u32[]{:S(2)}) copy-start(f32[2,128,128]{2,1,0:T(8,128)S(1)} %get-tuple-element.25) | copy-start | bytes 393220
  68.5 8.0 %copy-start.11 = (f32[2,1,128,128]{2,3,1,0:T(8,128)}, f32[2,1,128,128]{2,3,1,0:T(8,128)S(1)}, u32[]{:S(2)}) copy-start(f32[2,1,128,128]{2,3,1,0:T(8,128)S(1)} %custom-call.25) | copy-start | bytes 393220
  71.9 7.1 %copy-start.19 = (f32[128,256]{1,0:T(8,128)S(1)}, f32[128,256]{1,0:T(8,128)}, u32[]{:S(2)}) copy-start(f32[128,256]{1,0:T(8,128)} %param.20) | copy-start | bytes 393220
  71.9 8.2 %copy-start.25 = (s32[4]{0:T(128)S(1)}, s32[4]{0:T(128)}, u32[]{:S(2)}) copy-start(s32[4]{0:T(128)} %constant.336) | copy-start | bytes 52
  80.0 8.9 %collective-permute-start.11 = (f32[256,128]{1,0:T(8,128)S(1)}, f32[256,128]{1,0:T(8,128)S(1)}, u32[]{:S(2)}, u32[]{:S(2)}) collective-permute-start(f32[256,128]{1,0:T(8,128)S(1)} %slice.324), channel_id=1, source_target_pairs={{252,0},{253,1},{254,2},{255,3},{0,4},{1,5},{2,6},{3,7},{4,8},{5,9... | collective-permute-start | bytes 393224 | tf_op jit(solution)/shard_map/ppermute | solution.py:20
  80.1 9.2 %copy-start.14 = (f32[1,256,128]{2,1,0:T(8,128)}, f32[1,256,128]{2,1,0:T(8,128)S(1)}, u32[]{:S(2)}) copy-start(f32[1,256,128]{2,1,0:T(8,128)S(1)} %collective-permute-done.7) | copy-start | bytes 393220
  80.2 9.2 %copy-start.16 = (f32[1,256,128]{2,1,0:T(8,128)}, f32[1,256,128]{2,1,0:T(8,128)S(1)}, u32[]{:S(2)}) copy-start(f32[1,256,128]{2,1,0:T(8,128)S(1)} %collective-permute-done.6) | copy-start | bytes 393220
  82.0 34.9 %collective-permute-start.8 = (f32[3,256,128]{2,1,0:T(8,128)}, f32[3,256,128]{2,1,0:T(8,128)}, u32[]{:S(2)}, u32[]{:S(2)}) collective-permute-start(f32[3,256,128]{2,1,0:T(8,128)} %pad_maximum_fusion.1), channel_id=1, source_target_pairs={{253,0},{254,1},{255,2},{0,3},{1,4},{2,5},{3,6},{4,7},{5,8},{6,9},... | collective-permute-start | bytes 1179656 | tf_op jit(solution)/shard_map/ppermute | solution.py:20
  82.0 36.0 %collective-permute-start.9 = (f32[3,256,128]{2,1,0:T(8,128)}, f32[3,256,128]{2,1,0:T(8,128)}, u32[]{:S(2)}, u32[]{:S(2)}) collective-permute-start(f32[3,256,128]{2,1,0:T(8,128)} %pad_maximum_fusion.1), channel_id=1, source_target_pairs={{3,0},{4,1},{5,2},{6,3},{7,4},{8,5},{9,6},{10,7},{11,8},{12,9},{13... | collective-permute-start | bytes 1179656 | tf_op jit(solution)/shard_map/ppermute | solution.py:20
  88.9 10.2 %collective-permute-start.12 = (f32[256,128]{1,0:T(8,128)S(1)}, f32[256,128]{1,0:T(8,128)S(1)}, u32[]{:S(2)}, u32[]{:S(2)}) collective-permute-start(f32[256,128]{1,0:T(8,128)S(1)} %slice.324), channel_id=1, source_target_pairs={{254,0},{255,1},{0,2},{1,3},{2,4},{3,5},{4,6},{5,7},{6,8},{7,9},{8... | collective-permute-start | bytes 393224 | tf_op jit(solution)/shard_map/ppermute | solution.py:20
  89.3 28.6 %copy-start.17 = (f32[1,256,128]{2,1,0:T(8,128)S(1)}, f32[1,256,128]{2,1,0:T(8,128)}, u32[]{:S(2)}) copy-start(f32[1,256,128]{2,1,0:T(8,128)} %copy-done.16) | copy-start | bytes 393220
  89.4 28.6 %copy-start.3 = (f32[1,256,256]{2,1,0:T(8,128)S(1)}, f32[1,256,256]{2,1,0:T(8,128)}, u32[]{:S(2)}) copy-start(f32[1,256,256]{2,1,0:T(8,128)} %param.19) | copy-start | bytes 786436
  89.4 28.5 %copy-start.7 = (f32[2,256,128]{2,1,0:T(8,128)}, f32[2,256,128]{2,1,0:T(8,128)S(1)}, u32[]{:S(2)}) copy-start(f32[2,256,128]{2,1,0:T(8,128)S(1)} %collective-permute-done.1) | copy-start | bytes 786436
  89.4 12.3 %collective-permute-start.13 = (f32[256,128]{1,0:T(8,128)S(1)}, f32[256,128]{1,0:T(8,128)S(1)}, u32[]{:S(2)}, u32[]{:S(2)}) collective-permute-start(f32[256,128]{1,0:T(8,128)S(1)} %slice.324), channel_id=1, source_target_pairs={{2,0},{3,1},{4,2},{5,3},{6,4},{7,5},{8,6},{9,7},{10,8},{11,9},{12,... | collective-permute-start | bytes 393224 | tf_op jit(solution)/shard_map/ppermute | solution.py:20
  96.5 21.4 %copy-start.9 = (f32[2,256,128]{2,1,0:T(8,128)}, f32[2,256,128]{2,1,0:T(8,128)S(1)}, u32[]{:S(2)}) copy-start(f32[2,256,128]{2,1,0:T(8,128)S(1)} %collective-permute-done) | copy-start | bytes 786436
  96.5 18.9 %collective-permute-start.14 = (f32[256,128]{1,0:T(8,128)S(1)}, f32[256,128]{1,0:T(8,128)S(1)}, u32[]{:S(2)}, u32[]{:S(2)}) collective-permute-start(f32[256,128]{1,0:T(8,128)S(1)} %slice.324), channel_id=1, source_target_pairs={{4,0},{5,1},{6,2},{7,3},{8,4},{9,5},{10,6},{11,7},{12,8},{13,9},{1... | collective-permute-start | bytes 393224 | tf_op jit(solution)/shard_map/ppermute | solution.py:20
  97.5 20.5 %copy-start.15 = (f32[1,256,128]{2,1,0:T(8,128)S(1)}, f32[1,256,128]{2,1,0:T(8,128)}, u32[]{:S(2)}) copy-start(f32[1,256,128]{2,1,0:T(8,128)} %copy-done.14) | copy-start | bytes 393220
  99.1 21.7 %collective-permute-start.2 = (f32[6,256,128]{2,1,0:T(8,128)}, f32[6,256,128]{2,1,0:T(8,128)}, u32[]{:S(2)}, u32[]{:S(2)}) collective-permute-start(f32[6,256,128]{2,1,0:T(8,128)} %pad_maximum_fusion), channel_id=1, source_target_pairs={{253,0},{254,1},{255,2},{0,3},{1,4},{2,5},{3,6},{4,7},{5,8},{6,9},... | collective-permute-start | bytes 2359304 | tf_op jit(solution)/shard_map/ppermute | solution.py:20
  101.7 21.4 %collective-permute-start.3 = (f32[6,256,128]{2,1,0:T(8,128)}, f32[6,256,128]{2,1,0:T(8,128)}, u32[]{:S(2)}, u32[]{:S(2)}) collective-permute-start(f32[6,256,128]{2,1,0:T(8,128)} %pad_maximum_fusion), channel_id=1, source_target_pairs={{3,0},{4,1},{5,2},{6,3},{7,4},{8,5},{9,6},{10,7},{11,8},{12,9},{13... | collective-permute-start | bytes 2359304 | tf_op jit(solution)/shard_map/ppermute | solution.py:20
  120.8 2.2 copy-start.8
  127.1 5.8 %copy-start.22 = (pred[2,16]{1,0:T(4,128)(4,1)S(1)}, pred[2,16]{1,0:T(4,128)(4,1)}, u32[]{:S(2)}) copy-start(pred[2,16]{1,0:T(4,128)(4,1)} %get-tuple-element.26) | copy-start | bytes 100
  150.5 1.4 copy-start.12
  156.6 2.0 copy-start.20
  158.6 7.0 %copy-start.13 = (f32[2,128,128]{2,1,0:T(8,128)S(1)}, f32[2,128,128]{2,1,0:T(8,128)}, u32[]{:S(2)}) copy-start(f32[2,128,128]{2,1,0:T(8,128)} %convolution_subtract_fusion) | copy-start | bytes 393220
  158.6 7.0 %copy-start.23 = (f32[2,2]{1,0:T(2,128)S(1)}, f32[2,2]{1,0:T(2,128)}, u32[]{:S(2)}) copy-start(f32[2,2]{1,0:T(2,128)} %compare_convert_fusion.1) | copy-start | bytes 52
  163.6 2.0 copy-start
  200.2 20.2 %copy-start.2 = (f32[128,128]{1,0:T(8,128)}, f32[128,128]{1,0:T(8,128)S(1)}, u32[]{:S(2)}) copy-start(f32[128,128]{1,0:T(8,128)S(1)} %get-tuple-element.23) | copy-start | bytes 196612
  211.8 1.2 copy-start.4
  217.9 13.5 %collective-permute-start.10 = (f32[8,128,128]{1,2,0:T(8,128)S(1)}, f32[8,128,128]{1,2,0:T(8,128)S(1)}, u32[]{:S(2)}, u32[]{:S(2)}) collective-permute-start(f32[8,128,128]{1,2,0:T(8,128)S(1)} %fusion.16), channel_id=1, source_target_pairs={{0,1},{1,0},{2,3},{3,2},{4,5},{5,4},{6,7},{7,6},{8,9},{9,8},{10,11... | collective-permute-start | bytes 1572872 | tf_op jit(solution)/shard_map/ppermute | solution.py:26
  218.3 13.1 %collective-permute-start.5 = (f32[128,128]{0,1:T(8,128)S(1)}, f32[128,128]{0,1:T(8,128)S(1)}, u32[]{:S(2)}, u32[]{:S(2)}) collective-permute-start(f32[128,128]{0,1:T(8,128)S(1)} %convolution_subtract_fusion.1), channel_id=1, source_target_pairs={{0,1},{1,0},{2,3},{3,2},{4,5},{5,4},{6,7},{7,6},{8,9},{9,8},{10,11... | collective-permute-start | bytes 196616 | tf_op jit(solution)/shard_map/ppermute | solution.py:26
  232.2 24.2 %copy-start.18 = (f32[128,128]{0,1:T(8,128)S(1)}, f32[128,128]{0,1:T(8,128)}, u32[]{:S(2)}) copy-start(f32[128,128]{0,1:T(8,128)} %get-tuple-element.51) | copy-start | bytes 196612
  232.4 24.1 %copy-start.6 = (f32[4,256,128]{2,1,0:T(8,128)S(1)}, f32[4,256,128]{2,1,0:T(8,128)}, u32[]{:S(2)}) copy-start(f32[4,256,128]{2,1,0:T(8,128)} %gather_fusion.2) | copy-start | bytes 1572868
where the time goes:
time: 310 us; the launch traced here: 306 us
  other arithmetic  98.5 us (32%)
  local copies, waits for them, and re-layouts  60.3 us (19%)
  starting transfers between devices  43.2 us (14%)
  matrix products  41.5 us (13%)
  blocking collectives  41 us (13%)
  waiting for transfers between devices  17.2 us (6%)
  between operations  3.93 us (1%)
    another operation x10, other arithmetic, factor_box(): factor = jnp.linalg.cholesky(turned[:redundant, :redundant])  48.4 us
    psum x4, blocking collectives, by_axis(): value = lax.psum(value, axis)  41 us
    another operation x6, other arithmetic, factor_box(): jax.scipy.linalg.solve_triangular(factor, turned[:redundant, redundant:],...  40.7 us
    ppermute x12, starting transfers between devices, shifted(): return lax.ppermute(block, axis, route)  33.7 us
    dot_general x17, matrix products, product(): return jnp.matmul(left, right, precision=highest)  32.2 us
    slice x9, local copies, waits for them, and re-layouts, level_couplings(): chosen = jnp.stack([blocks[offset_slot] for offset_slot in offsets])  11.4 us
    ppermute x3, starting transfers between devices, from_partner(): return lax.ppermute(value, axis, pairs)  9.51 us
    ppermute x12, waiting for transfers between devices, shifted(): return lax.ppermute(block, axis, route)  9.41 us
  transfers between devices with their start and end apart: 15, of which 4 were waited for; matrix products, arithmetic and copies ran while one was open for 24% of the time, Pallas kernels for 0%

commit v1 on v0

v1 whole, which is shorter than its diff:
```python
import functools

import jax
import jax.numpy as jnp
from jax import lax
from jax.experimental import pallas as pl
from jax.experimental.pallas import tpu as pltpu
from jax.sharding import PartitionSpec as P

LEAF = 256
RANK = 128
NEAR = 16
AXES = ("grp", "leaf")
f32 = jnp.float32
bf16 = jnp.bfloat16
MESH = pl.DeviceIdType.MESH


def split(x):
    hi = x.astype(bf16)
    return hi, (x - hi.astype(f32)).astype(bf16)


def dg(a, b, ca, cb):
    return lax.dot_general(
        a, b, (((ca,), (cb,)), ((), ())), preferred_element_type=f32
    )


def dot3(a, b, ca=1, cb=0):
    ah, al = split(a)
    bh, bl = split(b)
    return dg(ah, bh, ca, cb) + (dg(ah, bl, ca, cb) + dg(al, bh, ca, cb))


def outer3(v, r):
    vh, vl = split(v)
    rh, rl = split(r)
    left = jnp.concatenate([vh, vl], axis=0)
    right = jnp.concatenate([rh, rh], axis=0)
    return dg(left, right, 0, 0) + dg(vh, rl, 0, 0)


def rowb(x, j):
    return jnp.broadcast_to(x[j : j + 1, :], x.shape)


def lane(x, i):
    return jnp.take_along_axis(x, jnp.full((8, 128), i, jnp.int32), axis=1)


def recip(b):
    r = pl.reciprocal(b, approx=True)
    r = r * (2.0 - b * r)
    return r * (2.0 - b * r)


def rsqrt(d):
    s = lax.rsqrt(d)
    return s * (1.5 - (0.5 * d) * (s * s))


def eliminate(A, VE, D, n):
    row = lax.broadcasted_iota(jnp.int32, (8, 128), 0)

    def body(k, carry):
        kk = pl.multiple_of(8 * k, 8)
        kn = pl.multiple_of(8 * jnp.minimum(k + 1, 15), 8)
        state = []
        for i in range(n):
            c0, c1, v0, v1, rr = carry[i]
            scaled = jnp.concatenate([v0 * rr, v1 * rr], axis=1)
            A[i] = A[i] - outer3(v0, scaled)
            nxt = A[i, pl.ds(kn, 8), :]
            n0, n1 = nxt[:, :128], nxt[:, 128:]
            cb = [lane(c0, kk + j) for j in range(8)]
            nb = [lane(n0, kk + j) for j in range(8)]
            one = jnp.ones_like(c0)
            state.append([c0, c1, n0, n1, cb, nb, c0, c1, one, one])
        for j in range(8):
            for i in range(n):
                x0, x1, n0, n1, cb, nb, v0, v1, d, rr = state[i]
                b = rowb(cb[j], j)
                r = recip(b)
                here = row == j
                m = jnp.where(here, 0.0, cb[j] * r)
                v0 = jnp.where(here, x0, v0)
                v1 = jnp.where(here, x1, v1)
                d = jnp.where(here, b, d)
                rr = jnp.where(here, r, rr)
                cb = [cb[q] - m * rowb(cb[q], j) if q > j else cb[q] for q in range(8)]
                x0 = x0 - m * rowb(x0, j)
                x1 = x1 - m * rowb(x1, j)
                state[i] = [x0, x1, n0, n1, cb, nb, v0, v1, d, rr]
        result = []
        for i in range(n):
            x0, x1, n0, n1, cb, nb, v0, v1, d, rr = state[i]
            p0, p1 = x0 * rr, x1 * rr
            for j in range(8):
                n0 = n0 - nb[j] * rowb(p0, j)
                n1 = n1 - nb[j] * rowb(p1, j)
            VE[i, pl.ds(kk, 8), :] = jnp.concatenate([v0, v1], axis=1)
            D[i, pl.ds(kk, 8), :] = d
            result.append((n0, n1, v0, v1, rr))
        return tuple(result)

    zero = jnp.zeros((8, 128), f32)
    start = tuple((A[i, 0:8, :128], A[i, 0:8, 128:], zero, zero, zero) for i in range(n))
    lax.fori_loop(0, 16, body, start)


def load_system(A, i, y_rr):
    rows = lax.broadcasted_iota(jnp.int32, (RANK, RANK), 0)
    cols = lax.broadcasted_iota(jnp.int32, (RANK, RANK), 1)
    A[i, :, :RANK] = y_rr
    A[i, :, RANK:] = (rows == cols).astype(f32)


def finish(VE, D, i, y, basis_t):
    rows = lax.broadcasted_iota(jnp.int32, (RANK, RANK), 0)
    cols = lax.broadcasted_iota(jnp.int32, (RANK, RANK), 1)
    d = D[i]
    s = rsqrt(d)
    upper = jnp.where(cols >= rows, VE[i, :, :RANK] * s, 0.0)
    inverse = VE[i, :, RANK:] * s
    xh = dot3(inverse, jnp.concatenate([y[:RANK, RANK:], basis_t[:RANK]], axis=1))
    sa = jnp.concatenate([y[RANK:, RANK:], basis_t[RANK:]], axis=1) - dot3(
        xh[:, :RANK], xh, 0, 0
    )
    return upper.T, sa[:, :RANK], sa[:, RANK:]


def log_rows(d):
    return jnp.sum(jnp.log(d), axis=0, keepdims=True)


def block_system(s0, c01, c10, s1):
    return jnp.concatenate(
        [
            jnp.concatenate([s0, 0.5 * (c01 + c10.T)], axis=1),
            jnp.concatenate([0.5 * (c01.T + c10), s1], axis=1),
        ],
        axis=0,
    )


def kernel(
    groups,
    leaves,
    near,
    diag,
    leaf_basis,
    basis1,
    basis2,
    ids,
    mask,
    F0,
    F1,
    F2,
    S2,
    C2,
    LD,
    nv,
    dv,
    bv,
    b1v,
    wv,
    bt,
    yv,
    tu,
    win,
    zown,
    zsib,
    zu,
    at,
    A,
    VE,
    D,
    ex,
    vf,
    f2,
    la,
    lg,
    load_sem,
    send_sem,
    recv_sem,
    la_send,
    la_recv,
    lg_send,
    lg_recv,
):
    count = groups * leaves
    g = lax.axis_index("grp")
    l = lax.axis_index("leaf")
    m = g * leaves + l
    par = lax.rem(m, 2)

    def device(k):
        return (k // leaves, lax.rem(k, leaves))

    def shifted(delta):
        return lax.rem(m + (delta + count), count)

    sibling = m + 1 - 2 * par

    loads = [
        pltpu.make_async_copy(leaf_basis, bv, load_sem.at[0]),
        pltpu.make_async_copy(basis1.at[0], b1v, load_sem.at[1]),
        pltpu.make_async_copy(basis2, wv.at[par], load_sem.at[2]),
        pltpu.make_async_copy(diag, dv, load_sem.at[3]),
        pltpu.make_async_copy(near, nv, load_sem.at[4]),
    ]
    for copy in loads:
        copy.start()

    barrier = pltpu.get_barrier_semaphore()
    deltas = (-1, 1, -2, 2, -3, 3, -4, 4)
    for delta in deltas:
        pl.semaphore_signal(barrier, inc=1, device_id=device(shifted(delta)), device_id_type=MESH)

    def greet_leaf(t, _):
        pl.semaphore_signal(
            barrier, inc=1, device_id=(g, lax.rem(l + t, leaves)), device_id_type=MESH
        )
        return 0

    def greet_group(t, _):
        pl.semaphore_signal(
            barrier, inc=1, device_id=(lax.rem(g + t, groups), l), device_id_type=MESH
        )
        return 0

    lax.fori_loop(1, leaves, greet_leaf, 0)
    lax.fori_loop(1, groups, greet_group, 0)

    for copy in loads[:3]:
        copy.wait()
    q2 = wv[par, :, RANK:]
    for b in range(2):
        t = dot3(bv[b, :, RANK:], b1v[b * RANK : (b + 1) * RANK, RANK:])
        tu[1, b] = t
        tu[0, b] = dot3(t, q2)

    pl.semaphore_wait(barrier, 8 + (leaves - 1) + (groups - 1))
    sends = []
    for k, delta in enumerate(deltas):
        target = shifted(delta)
        kind = jnp.where(target == sibling, 1, 0)
        sends.append(
            pltpu.make_async_remote_copy(
                src_ref=tu.at[kind],
                dst_ref=win.at[4 - delta],
                send_sem=send_sem.at[k],
                recv_sem=recv_sem.at[4 - delta],
                device_id=device(target),
                device_id_type=MESH,
            )
        )
    w_send = pltpu.make_async_remote_copy(
        src_ref=wv.at[par],
        dst_ref=wv.at[par],
        send_sem=send_sem.at[8],
        recv_sem=recv_sem.at[9],
        device_id=device(sibling),
        device_id_type=MESH,
    )
    w_send.start()
    for copy in sends:
        copy.start()

    loads[3].wait()
    for i in range(2):
        bt[i] = bv[i].T
        y = dot3(bt[i], dot3(dv[i], bv[i]))
        yv[i] = y
        load_system(A, i, y[:RANK, :RANK])
    eliminate(A, VE, D, 2)
    loads[4].wait()

    def near_block(a, j):
        slot = jnp.int32(0)
        live = f32(0.0)
        for t in range(NEAR):
            hit = jnp.logical_and(ids[a, t] == j, mask[a, t] == 1)
            slot = jnp.where(hit, t, slot)
            live = jnp.where(hit, f32(1.0), live)
        return nv[a * NEAR + slot], live

    schur = []
    logs = jnp.zeros((1, RANK), f32)
    for i in range(2):
        lower, s, a_t = finish(VE, D, i, yv[i], bt[i])
        F0[i] = lower
        at[i] = a_t
        schur.append(s)
        logs = logs + log_rows(D[i])
        tile, live = near_block(i, 2 * m + 1 - i)
        zown[i] = dot3(tile, bv[1 - i, :, RANK:] * live)

    system = block_system(schur[0], dot3(at[0], zown[0]), dot3(at[1], zown[1]), schur[1])
    bt[0] = b1v[...].T
    y = dot3(bt[0], dot3(system, b1v[...]))
    yv[0] = y
    load_system(A, 0, y[:RANK, :RANK])
    eliminate(A, VE, D, 1)

    def arrived(slot):
        pltpu.make_async_copy(win.at[slot], win.at[slot], recv_sem.at[slot]).wait()

    for delta in deltas:
        arrived(4 + delta)

    for i in range(2):
        z = jnp.zeros((LEAF, RANK), f32)
        for c in range(2):
            tile, live = near_block(i, 2 * sibling + c)
            z = z + dot3(tile, win[5 - 2 * par, c] * live)
        zsib[i * RANK : (i + 1) * RANK] = dot3(at[i], z)

    lower, s, a1_t = finish(VE, D, 0, yv[0], bt[0])
    F1[0] = lower
    logs = logs + log_rows(D[0])
    ex[par, 0] = s
    ex[par, 1] = dot3(a1_t, zsib[...])
    ex_send = pltpu.make_async_remote_copy(
        src_ref=ex.at[par],
        dst_ref=ex.at[par],
        send_sem=send_sem.at[9],
        recv_sem=recv_sem.at[10],
        device_id=device(sibling),
        device_id_type=MESH,
    )
    ex_send.start()

    def far(step, _):
        a = step // 4
        slot_e = lax.rem(step, 4)
        e = slot_e - 2 + slot_e // 2
        z = jnp.zeros((LEAF, RANK), f32)
        for c in range(4):
            tile, live = near_block(a, 4 * (m // 2) + 4 * e + c)
            source = jnp.clip(2 * e + c // 2 - par + 4, 0, 8)
            z = z + dot3(tile, win[source, c % 2] * live)
        zu[slot_e, pl.ds(pl.multiple_of(a * RANK, RANK), RANK)] = dot3(at[a], z)
        return 0

    win[4] = jnp.zeros((2, LEAF, RANK), f32)
    lax.fori_loop(0, 8, far, 0)
    vf[par] = dot3(a1_t, jnp.concatenate([zu[e] for e in range(4)], axis=1))
    v_send = pltpu.make_async_remote_copy(
        src_ref=vf.at[par],
        dst_ref=vf.at[par],
        send_sem=send_sem.at[10],
        recv_sem=recv_sem.at[11],
        device_id=device(sibling),
        device_id_type=MESH,
    )
    v_send.start()

    w_send.wait()
    w = jnp.concatenate([wv[0], wv[1]], axis=0)
    bt[0] = w.T
    ex_send.wait()
    system = block_system(ex[0, 0], ex[0, 1], ex[1, 1], ex[1, 0])
    y = dot3(bt[0], dot3(system, w))
    yv[0] = y
    load_system(A, 0, y[:RANK, :RANK])
    eliminate(A, VE, D, 1)
    logs = logs + log_rows(D[0]) * jnp.where(par == 0, 1.0, 0.0)
    la[l] = jnp.broadcast_to(logs, (8, RANK))

    def to_leaf(t, wait):
        copy = pltpu.make_async_remote_copy(
            src_ref=la.at[l],
            dst_ref=la.at[l],
            send_sem=la_send.at[t],
            recv_sem=la_recv.at[t],
            device_id=(g, lax.rem(l + t, leaves)),
            device_id_type=MESH,
        )
        if wait:
            copy.wait()
        else:
            copy.start()

    def to_group(t, wait):
        copy = pltpu.make_async_remote_copy(
            src_ref=lg.at[g],
            dst_ref=lg.at[g],
            send_sem=lg_send.at[t],
            recv_sem=lg_recv.at[t],
            device_id=(lax.rem(g + t, groups), l),
            device_id_type=MESH,
        )
        if wait:
            copy.wait()
        else:
            copy.start()

    def each(size, step, wait):
        def body(t, _):
            step(t, wait)
            return 0

        lax.fori_loop(1, size, body, 0)

    each(leaves, to_leaf, False)
    lower, s, a2_t = finish(VE, D, 0, yv[0], bt[0])
    half = pl.multiple_of(par * (RANK // 2), RANK // 2)
    f2[:, :RANK] = lower
    f2[:, RANK : 2 * RANK] = s
    f2[:, 2 * RANK :] = a2_t
    F2[...] = f2[pl.ds(half, RANK // 2), :RANK]
    S2[...] = f2[pl.ds(half, RANK // 2), RANK : 2 * RANK]
    each(leaves, to_leaf, True)
    lg[g] = jnp.sum(la[...], axis=0)
    each(groups, to_group, False)
    v_send.wait()
    C2[...] = dot3(
        f2[pl.ds(half, RANK // 2), 2 * RANK :], jnp.concatenate([vf[0], vf[1]], axis=0)
    )
    for copy in sends:
        copy.wait_send()
    each(groups, to_group, True)
    LD[...] = jnp.sum(lg[...], axis=0)


def on_device(
    near_tiles, diag_tiles, near_index, near_mask, leaf_basis, level1_basis, level2_basis
):
    groups, leaves = lax.axis_size("grp"), lax.axis_size("leaf")
    any_spec = pl.BlockSpec(memory_space=pl.ANY)
    smem = pl.BlockSpec(memory_space=pltpu.SMEM)
    vmem = pl.BlockSpec(memory_space=pltpu.VMEM)
    dma = pltpu.SemaphoreType.DMA
    outs = pl.pallas_call(
        functools.partial(kernel, groups, leaves),
        out_shape=(
            jax.ShapeDtypeStruct((2, RANK, RANK), f32),
            jax.ShapeDtypeStruct((1, RANK, RANK), f32),
            jax.ShapeDtypeStruct((RANK // 2, RANK), f32),
            jax.ShapeDtypeStruct((RANK // 2, RANK), f32),
            jax.ShapeDtypeStruct((RANK // 2, 4 * RANK), f32),
            jax.ShapeDtypeStruct((8, RANK), f32),
        ),
        in_specs=[any_spec] * 5 + [smem] * 2,
        out_specs=[vmem] * 6,
        scratch_shapes=[
            pltpu.VMEM((2 * NEAR, LEAF, LEAF), f32),
            pltpu.VMEM((2, LEAF, LEAF), f32),
            pltpu.VMEM((2, LEAF, LEAF), f32),
            pltpu.VMEM((LEAF, LEAF), f32),
            pltpu.VMEM((2, RANK, LEAF), f32),
            pltpu.VMEM((2, LEAF, LEAF), f32),
            pltpu.VMEM((2, LEAF, LEAF), f32),
            pltpu.VMEM((2, 2, LEAF, RANK), f32),
            pltpu.VMEM((9, 2, LEAF, RANK), f32),
            pltpu.VMEM((2, LEAF, RANK), f32),
            pltpu.VMEM((LEAF, RANK), f32),
            pltpu.VMEM((4, LEAF, RANK), f32),
            pltpu.VMEM((2, RANK, LEAF), f32),
            pltpu.VMEM((2, RANK, 2 * RANK), f32),
            pltpu.VMEM((2, RANK, 2 * RANK), f32),
            pltpu.VMEM((2, RANK, RANK), f32),
            pltpu.VMEM((2, 2, RANK, RANK), f32),
            pltpu.VMEM((2, RANK, 4 * RANK), f32),
            pltpu.VMEM((RANK, 4 * RANK), f32),
            pltpu.VMEM((leaves, 8, RANK), f32),
            pltpu.VMEM((groups, 8, RANK), f32),
            dma((5,)),
            dma((11,)),
            dma((12,)),
            dma((leaves,)),
            dma((leaves,)),
            dma((groups,)),
            dma((groups,)),
        ],
        compiler_params=pltpu.CompilerParams(
            collective_id=0, has_side_effects=True, vmem_limit_bytes=48 << 20
        ),
    )(near_tiles.reshape(2 * NEAR, LEAF, LEAF), diag_tiles, leaf_basis, level1_basis, level2_basis, near_index, near_mask)
    return (*outs[:5], outs[5][0, 0])


def solution(mesh):
    in_specs = (
        P(AXES, None, None, None),
        P(AXES, None, None),
        P(AXES, None),
        P(AXES, None),
        P(AXES, None, None),
        P(AXES, None, None),
        P(AXES, None),
    )
    out_specs = (
        P(AXES, None, None),
        P(AXES, None, None),
        P(AXES, None),
        P(AXES, None),
        P(AXES, None),
        P(),
    )
    return jax.shard_map(
        on_device, mesh=mesh, in_specs=in_specs, out_specs=out_specs, check_vma=False
    )
```

time: 310 us -> 77.8 us (0.25)
  the two profiles are of different devices: /device:TPU:2 before, /device:TPU:1 now
where the time goes in v1:
time: 77.8 us; the launch traced here: 77.6 us
  Pallas kernels  67.9 us (87%)
  local copies, waits for them, and re-layouts  8.97 us (12%)
    pallas_call x1, Pallas kernels, on_device(): pl.pallas_call(functools.partial(kernel, groups, leaves), out_shape=(jax....  67.9 us
    unnamed x17, local copies, waits for them, and re-layouts  8.45 us

profile of v1, /device:TPU:1, one launch (start us, length us, event | category | flops | bytes accessed | tf_op | source)
XLA Modules:
  0.0 77.6 jit_solution(3455318599754718104)
XLA Ops:
  0.6 0.0 copy-start
  0.6 1.0 %copy-done = f32[2,256,256]{2,1,0:T(8,128)S(1)} copy-done((f32[2,256,256]{2,1,0:T(8,128)S(1)}, f32[2,256,256]{2,1,0:T(8,128)}, u32[]{:S(2)}) %copy-start) | copy-done | bytes 524312
  1.7 0.0 copy-start.1
  1.7 1.0 %copy-done.1 = f32[2,256,256]{2,1,0:T(8,128)S(1)} copy-done((f32[2,256,256]{2,1,0:T(8,128)S(1)}, f32[2,256,256]{2,1,0:T(8,128)}, u32[]{:S(2)}) %copy-start.1) | copy-done | bytes 524312
  2.7 0.0 copy-start.2
  2.7 0.9 %copy-done.2 = f32[1,256,256]{2,1,0:T(8,128)S(1)} copy-done((f32[1,256,256]{2,1,0:T(8,128)S(1)}, f32[1,256,256]{2,1,0:T(8,128)}, u32[]{:S(2)}) %copy-start.2) | copy-done | bytes 262168
  3.7 0.0 copy-start.3
  3.7 0.9 %copy-done.3 = f32[128,256]{1,0:T(8,128)S(1)} copy-done((f32[128,256]{1,0:T(8,128)S(1)}, f32[128,256]{1,0:T(8,128)}, u32[]{:S(2)}) %copy-start.3) | copy-done | bytes 131096
  4.6 0.0 copy-start.4
  4.6 0.7 copy-done.4
  5.3 0.0 copy-start.5
  5.3 0.7 copy-done.5
  5.9 67.9 %shard_map.118 = (f32[2,128,128]{2,1,0:T(8,128)S(1)}, f32[1,128,128]{2,1,0:T(8,128)S(1)}, f32[64,128]{1,0:T(8,128)S(1)}, f32[64,128]{1,0:T(8,128)S(1)}, f32[64,512]{1,0:T(8,128)S(1)}, /*index=5*/f32[8,128]{1,0:T(8,128)S(1)}) custom-call(f32[32,256,256]{2,1,0:T(8,128)} %bitcast.2, f32[2,256,256]{2,1,0:T(8,128)S(1)} %copy-done, f32[2,256,256]{2,1,0:T(8,128)S(1)} %copy-done.1, ...), custom_call_target="tpu_custom_call" | custom-call | tf_op jit(solution)/shard_map/pallas_call | solution.py:436
  73.9 0.5 slice.3
  74.4 0.7 copy.18
  75.1 0.6 copy.19
  75.7 0.6 copy.20
  76.3 0.6 copy.21
  76.9 0.7 copy.22
Async XLA Ops:
  0.6 1.0 %copy-start = (f32[2,256,256]{2,1,0:T(8,128)S(1)}, f32[2,256,256]{2,1,0:T(8,128)}, u32[]{:S(2)}) copy-start(f32[2,256,256]{2,1,0:T(8,128)} %diag.1) | copy-start | bytes 1572868
  1.7 1.0 %copy-start.1 = (f32[2,256,256]{2,1,0:T(8,128)S(1)}, f32[2,256,256]{2,1,0:T(8,128)}, u32[]{:S(2)}) copy-start(f32[2,256,256]{2,1,0:T(8,128)} %leaf_basis.1) | copy-start | bytes 1572868
  2.7 0.9 %copy-start.2 = (f32[1,256,256]{2,1,0:T(8,128)S(1)}, f32[1,256,256]{2,1,0:T(8,128)}, u32[]{:S(2)}) copy-start(f32[1,256,256]{2,1,0:T(8,128)} %basis1.1) | copy-start | bytes 786436
  3.7 0.9 %copy-start.3 = (f32[128,256]{1,0:T(8,128)S(1)}, f32[128,256]{1,0:T(8,128)}, u32[]{:S(2)}) copy-start(f32[128,256]{1,0:T(8,128)} %basis2.1) | copy-start | bytes 393220
  4.6 0.7 copy-start.4
  5.3 0.7 copy-start.5

commit v2 on v1

v2 whole, which is shorter than its diff:
```python
import functools

import jax
import jax.numpy as jnp
from jax import lax
from jax.experimental import pallas as pl
from jax.experimental.pallas import tpu as pltpu
from jax.sharding import PartitionSpec as P

LEAF = 256
RANK = 128
NEAR = 16
AXES = ("grp", "leaf")
f32 = jnp.float32
bf16 = jnp.bfloat16
MESH = pl.DeviceIdType.MESH


def split(x):
    hi = x.astype(bf16)
    return hi, (x - hi.astype(f32)).astype(bf16)


def dg(a, b, ca, cb):
    return lax.dot_general(
        a, b, (((ca,), (cb,)), ((), ())), preferred_element_type=f32
    )


def dot3(a, b, ca=1, cb=0):
    ah, al = split(a)
    bh, bl = split(b)
    return dg(ah, bh, ca, cb) + (dg(ah, bl, ca, cb) + dg(al, bh, ca, cb))


def outer3(v, r):
    vh, vl = split(v)
    rh, rl = split(r)
    left = jnp.concatenate([vh, vl], axis=0)
    right = jnp.concatenate([rh, rh], axis=0)
    return dg(left, right, 0, 0) + dg(vh, rl, 0, 0)


def rowb(x, j):
    return jnp.broadcast_to(x[j : j + 1, :], x.shape)


def lane(x, i):
    return jnp.take_along_axis(x, jnp.full((8, 128), i, jnp.int32), axis=1)


def rsqrt(d):
    s = lax.rsqrt(d)
    return s * (1.5 - (0.5 * d) * (s * s))


def dot3n(a, b):
    ah, al = split(a)
    bh, bl = split(b)
    wide = dg(ah, jnp.concatenate([bh, bl], axis=1), 1, 0)
    n = b.shape[1]
    return wide[:, :n] + (wide[:, n:] + dg(al, bh, 1, 0))


def pivots(state, n):
    row = lax.broadcasted_iota(jnp.int32, (8, 128), 0)
    one = jnp.ones((8, 128), f32)
    full = [[x0, x1, cb, x0, x1, one, one] for x0, x1, cb in state]
    for j in range(8):
        for i in range(n):
            x0, x1, cb, v0, v1, d, rr = full[i]
            b = rowb(cb[j], j)
            r0 = pl.reciprocal(b, approx=True)
            e = 2.0 - b * r0
            r = r0 * e
            e = 2.0 - b * r
            here = row == j
            m = jnp.where(here, 0.0, cb[j] * r) * e
            v0 = jnp.where(here, x0, v0)
            v1 = jnp.where(here, x1, v1)
            d = jnp.where(here, b, d)
            rr = jnp.where(here, r * e, rr)
            cb = [cb[q] - m * rowb(cb[q], j) if q > j else cb[q] for q in range(8)]
            x0 = x0 - m * rowb(x0, j)
            x1 = x1 - m * rowb(x1, j)
            full[i] = [x0, x1, cb, v0, v1, d, rr]
    return full


def eliminate(A, VE, D, n):
    ahead = n == 1

    def body(k, carry):
        kk = pl.multiple_of(8 * k, 8)
        kn = pl.multiple_of(8 * jnp.minimum(k + 1, 15), 8)
        before = 8 * jnp.maximum(k - 1, 0)
        state = []
        rest = []
        for i in range(n):
            c0, c1, v0, v1, rr, p0, p1 = carry[i]
            scaled = jnp.concatenate([v0 * rr, v1 * rr], axis=1)
            if ahead:
                nxt = A[i, pl.ds(kn, 8), :]
                A[i] = A[i] - outer3(v0, scaled)
            else:
                A[i] = A[i] - outer3(v0, scaled)
                nxt = A[i, pl.ds(kn, 8), :]
            n0, n1 = nxt[:, :128], nxt[:, 128:]
            cb = [lane(c0, kk + j) for j in range(8)]
            if ahead:
                fb = [lane(n0, before + j) for j in range(8)]
                for j in range(8):
                    n0 = n0 - fb[j] * rowb(p0, j)
                    n1 = n1 - fb[j] * rowb(p1, j)
            nb = [lane(n0, kk + j) for j in range(8)]
            state.append([c0, c1, cb])
            rest.append([n0, n1, nb])
        full = pivots(state, n)
        result = []
        for i in range(n):
            x0, x1, _, v0, v1, d, rr = full[i]
            n0, n1, nb = rest[i]
            p0, p1 = x0 * rr, x1 * rr
            for j in range(8):
                n0 = n0 - nb[j] * rowb(p0, j)
                n1 = n1 - nb[j] * rowb(p1, j)
            VE[i, pl.ds(kk, 8), :] = jnp.concatenate([v0, v1], axis=1)
            D[i, pl.ds(kk, 8), :] = d
            result.append((n0, n1, v0, v1, rr, p0, p1))
        return tuple(result)

    zero = jnp.zeros((8, 128), f32)
    start = tuple((A[i, 0:8, :128], A[i, 0:8, 128:]) + (zero,) * 5 for i in range(n))
    lax.fori_loop(0, 16, body, start)


def load_system(A, i, y_rr):
    rows = lax.broadcasted_iota(jnp.int32, (RANK, RANK), 0)
    cols = lax.broadcasted_iota(jnp.int32, (RANK, RANK), 1)
    A[i, :, :RANK] = y_rr
    A[i, :, RANK:] = (rows == cols).astype(f32)


def finish(VE, D, i, y, basis_t):
    rows = lax.broadcasted_iota(jnp.int32, (RANK, RANK), 0)
    cols = lax.broadcasted_iota(jnp.int32, (RANK, RANK), 1)
    d = D[i]
    s = rsqrt(d)
    upper = jnp.where(cols >= rows, VE[i, :, :RANK] * s, 0.0)
    inverse = VE[i, :, RANK:] * s
    xh = dot3(inverse, jnp.concatenate([y[:RANK, RANK:], basis_t[:RANK]], axis=1))
    sa = jnp.concatenate([y[RANK:, RANK:], basis_t[RANK:]], axis=1) - dot3(
        xh[:, :RANK], xh, 0, 0
    )
    return upper.T, sa[:, :RANK], sa[:, RANK:]


def log_rows(d):
    return jnp.sum(jnp.log(d), axis=0, keepdims=True)


def block_system(s0, c01, c10, s1):
    return jnp.concatenate(
        [
            jnp.concatenate([s0, 0.5 * (c01 + c10.T)], axis=1),
            jnp.concatenate([0.5 * (c01.T + c10), s1], axis=1),
        ],
        axis=0,
    )


def kernel(
    groups,
    leaves,
    near,
    diag,
    leaf_basis,
    basis1,
    basis2,
    ids_hbm,
    mask_hbm,
    F0,
    F1,
    F2,
    S2,
    C2,
    LD,
    nv,
    dv,
    bv,
    b1v,
    wv,
    bt,
    yv,
    tu,
    us,
    win,
    zown,
    zsib,
    zu,
    at,
    A,
    VE,
    D,
    ex,
    pp,
    pr,
    f2,
    la,
    lg,
    ids,
    mask,
    load_sem,
    send_sem,
    recv_sem,
    la_send,
    la_recv,
    lg_send,
    lg_recv,
):
    count = groups * leaves
    g = lax.axis_index("grp")
    l = lax.axis_index("leaf")
    m = g * leaves + l
    par = lax.rem(m, 2)
    side = 2 * par - 1

    def device(k):
        return (k // leaves, lax.rem(k, leaves))

    def shifted(delta):
        return lax.rem(m + (delta + count), count)

    sibling = m - side

    loads = [
        pltpu.make_async_copy(leaf_basis, bv, load_sem.at[0]),
        pltpu.make_async_copy(basis1.at[0], b1v, load_sem.at[1]),
        pltpu.make_async_copy(basis2, wv.at[par], load_sem.at[2]),
        pltpu.make_async_copy(diag, dv, load_sem.at[3]),
        pltpu.make_async_copy(ids_hbm, ids, load_sem.at[4]),
        pltpu.make_async_copy(mask_hbm, mask, load_sem.at[5]),
        pltpu.make_async_copy(near, nv, load_sem.at[6]),
    ]
    for copy in loads[:4]:
        copy.start()

    barrier = pltpu.get_barrier_semaphore()
    direct = (-side, side, 3, -3, 4, -4)
    for delta in direct:
        pl.semaphore_signal(barrier, inc=1, device_id=device(shifted(delta)), device_id_type=MESH)

    def greet_leaf(t, _):
        pl.semaphore_signal(
            barrier, inc=1, device_id=(g, lax.rem(l + t, leaves)), device_id_type=MESH
        )
        return 0

    def greet_group(t, _):
        pl.semaphore_signal(
            barrier, inc=1, device_id=(lax.rem(g + t, groups), l), device_id_type=MESH
        )
        return 0

    lax.fori_loop(1, leaves, greet_leaf, 0)
    lax.fori_loop(1, groups, greet_group, 0)

    for copy in loads[:3]:
        copy.wait()
    for copy in loads[4:]:
        copy.start()
    q2 = wv[par, :, RANK:]
    for b in range(2):
        t = dot3(bv[b, :, RANK:], b1v[b * RANK : (b + 1) * RANK, RANK:])
        tu[1, b] = t
        tu[0, b] = dot3(t, q2)

    loads[3].wait()
    for i in range(2):
        bt[i] = bv[i].T
        y = dot3(bt[i], dot3(dv[i], bv[i]))
        yv[i] = y
        load_system(A, i, y[:RANK, :RANK])

    pl.semaphore_wait(barrier, len(direct) + (leaves - 1) + (groups - 1))

    def remote(src, dst, sent, received, target):
        return pltpu.make_async_remote_copy(
            src_ref=src,
            dst_ref=dst,
            send_sem=send_sem.at[sent],
            recv_sem=recv_sem.at[received],
            device_id=device(target),
            device_id_type=MESH,
        )

    w_send = remote(wv.at[par], wv.at[par], 6, 9, sibling)
    sends = []
    for k, delta in enumerate(direct):
        source = tu.at[1] if k == 0 else tu.at[0]
        sends.append(remote(source, win.at[4 - delta], k, 4 - delta, shifted(delta)))
    sends[0].start()
    sends[1].start()
    w_send.start()
    for copy in sends[2:]:
        copy.start()

    eliminate(A, VE, D, 2)
    for copy in loads[4:]:
        copy.wait()

    def near_block(a, j):
        slot = jnp.int32(0)
        live = f32(0.0)
        for t in range(NEAR):
            hit = jnp.logical_and(ids[a, t] == j, mask[a, t] == 1)
            slot = jnp.where(hit, t, slot)
            live = jnp.where(hit, f32(1.0), live)
        return nv[a * NEAR + slot], live

    schur = []
    logs = jnp.zeros((1, RANK), f32)
    for i in range(2):
        lower, s, a_t = finish(VE, D, i, yv[i], bt[i])
        F0[i] = lower
        at[i] = a_t
        schur.append(s)
        logs = logs + log_rows(D[i])
        tile, live = near_block(i, 2 * m + 1 - i)
        zown[i] = dot3n(tile, bv[1 - i, :, RANK:] * live)

    system = block_system(schur[0], dot3(at[0], zown[0]), dot3(at[1], zown[1]), schur[1])
    bt[0] = b1v[...].T
    y = dot3(bt[0], dot3(system, b1v[...]))
    yv[0] = y
    load_system(A, 0, y[:RANK, :RANK])

    def arrived(delta):
        slot = 4 + delta
        pltpu.make_async_copy(win.at[slot], win.at[slot], recv_sem.at[slot]).wait()

    arrived(side)
    relay_in = remote(win.at[4 + side], win.at[4 + 2 * side], 7, 4 + 2 * side, sibling)
    relay_in.start()
    eliminate(A, VE, D, 1)
    arrived(-side)

    for i in range(2):
        z = jnp.zeros((LEAF, RANK), f32)
        for c in range(2):
            tile, live = near_block(i, 2 * sibling + c)
            z = z + dot3n(tile, win[4 - side, c] * live)
        zsib[i * RANK : (i + 1) * RANK] = dot3(at[i], z)

    lower, s, a1_t = finish(VE, D, 0, yv[0], bt[0])
    F1[0] = lower
    logs = logs + log_rows(D[0])
    ex[par, 0] = s
    ex[par, 1] = dot3(a1_t, zsib[...])
    ex_send = remote(ex.at[par], ex.at[par], 9, 10, sibling)
    ex_send.start()

    w_send.wait_recv()
    q2 = wv[1 - par, :, RANK:]
    for b in range(2):
        us[b] = dot3(win[4 - side, b], q2)
    zu[...] = jnp.zeros_like(zu)
    w = jnp.concatenate([wv[0], wv[1]], axis=0)
    bt[0] = w.T
    relay_out = remote(us, win.at[4 - 2 * side], 8, 4 - 2 * side, shifted(side))
    relay_out.start()

    def far(delta):
        e = (par + delta + 8) // 2 - 4
        slot_e = jnp.where(e < 0, e + 2, e + 1)
        for a in range(2):
            z = zu[slot_e, a]
            for b in range(2):
                tile, live = near_block(a, 2 * (m + delta) + b)
                z = z + dot3n(tile, win[4 + delta, b] * live)
            zu[slot_e, a] = z

    far(side)
    arrived(4)
    far(4)

    ex_send.wait_recv()
    system = block_system(ex[0, 0], ex[0, 1], ex[1, 1], ex[1, 0])
    y = dot3(bt[0], dot3(system, w))
    yv[0] = y
    load_system(A, 0, y[:RANK, :RANK])
    eliminate(A, VE, D, 1)
    logs = logs + log_rows(D[0]) * jnp.where(par == 0, 1.0, 0.0)
    la[l] = jnp.broadcast_to(logs, (8, RANK))

    def to_leaf(t, wait):
        copy = pltpu.make_async_remote_copy(
            src_ref=la.at[l],
            dst_ref=la.at[l],
            send_sem=la_send.at[t],
            recv_sem=la_recv.at[t],
            device_id=(g, lax.rem(l + t, leaves)),
            device_id_type=MESH,
        )
        if wait:
            copy.wait()
        else:
            copy.start()

    def to_group(t, wait):
        copy = pltpu.make_async_remote_copy(
            src_ref=lg.at[g],
            dst_ref=lg.at[g],
            send_sem=lg_send.at[t],
            recv_sem=lg_recv.at[t],
            device_id=(lax.rem(g + t, groups), l),
            device_id_type=MESH,
        )
        if wait:
            copy.wait()
        else:
            copy.start()

    def each(size, step, wait):
        def body(t, _):
            step(t, wait)
            return 0

        lax.fori_loop(1, size, body, 0)

    each(leaves, to_leaf, False)
    lower, s, a2_t = finish(VE, D, 0, yv[0], bt[0])
    half = pl.multiple_of(par * (RANK // 2), RANK // 2)
    f2[:, :RANK] = lower
    f2[:, RANK:] = s
    F2[...] = f2[pl.ds(half, RANK // 2), :RANK]
    S2[...] = f2[pl.ds(half, RANK // 2), RANK:]
    chain = dot3(jnp.where(par == 0, a2_t[:, :RANK], a2_t[:, RANK:]), a1_t)
    for delta in (-4, 3, -3):
        arrived(delta)
        far(delta)
    each(leaves, to_leaf, True)
    lg[g] = jnp.sum(la[...], axis=0)
    each(groups, to_group, False)
    arrived(2 * side)
    far(2 * side)
    arrived(-2 * side)
    far(-2 * side)
    below = jnp.concatenate(
        [
            jnp.concatenate([dot3(at[a], zu[e, a]) for e in range(4)], axis=1)
            for a in range(2)
        ],
        axis=0,
    )
    part = dot3(chain, below)
    pp[0] = part[: RANK // 2]
    pp[1] = part[RANK // 2 :]
    p_send = remote(pp.at[1 - par], pr, 10, 11, sibling)
    p_send.start()
    for copy in sends:
        copy.wait_send()
    w_send.wait_send()
    ex_send.wait_send()
    relay_in.wait_send()
    relay_out.wait_send()
    p_send.wait()
    C2[...] = pp[par] + pr[...]
    each(groups, to_group, True)
    LD[...] = jnp.sum(lg[...], axis=0)


def write_out(*refs):
    sources, targets, ld, sem = refs[:5], refs[6:11], refs[11], refs[12]
    copies = [pltpu.make_async_copy(a, b, sem.at[i]) for i, (a, b) in enumerate(zip(sources, targets))]
    for copy in copies:
        copy.start()
    ld[0, 0] = refs[5][0, 0]
    for copy in copies:
        copy.wait()


def on_device(
    near_tiles, diag_tiles, near_index, near_mask, leaf_basis, level1_basis, level2_basis
):
    groups, leaves = lax.axis_size("grp"), lax.axis_size("leaf")
    hbm = pl.BlockSpec(memory_space=pltpu.HBM)
    vmem = pl.BlockSpec(memory_space=pltpu.VMEM)
    dma = pltpu.SemaphoreType.DMA
    shapes = (
        jax.ShapeDtypeStruct((2, RANK, RANK), f32),
        jax.ShapeDtypeStruct((1, RANK, RANK), f32),
        jax.ShapeDtypeStruct((RANK // 2, RANK), f32),
        jax.ShapeDtypeStruct((RANK // 2, RANK), f32),
        jax.ShapeDtypeStruct((RANK // 2, 4 * RANK), f32),
    )
    outs = pl.pallas_call(
        functools.partial(kernel, groups, leaves),
        out_shape=tuple(pltpu.VMEM(x.shape, f32) for x in shapes) + (pltpu.VMEM((8, RANK), f32),),
        in_specs=[hbm] * 7,
        out_specs=[vmem] * 6,
        scratch_shapes=[
            pltpu.VMEM((2 * NEAR, LEAF, LEAF), f32),
            pltpu.VMEM((2, LEAF, LEAF), f32),
            pltpu.VMEM((2, LEAF, LEAF), f32),
            pltpu.VMEM((LEAF, LEAF), f32),
            pltpu.VMEM((2, RANK, LEAF), f32),
            pltpu.VMEM((2, LEAF, LEAF), f32),
            pltpu.VMEM((2, LEAF, LEAF), f32),
            pltpu.VMEM((2, 2, LEAF, RANK), f32),
            pltpu.VMEM((2, LEAF, RANK), f32),
            pltpu.VMEM((9, 2, LEAF, RANK), f32),
            pltpu.VMEM((2, LEAF, RANK), f32),
            pltpu.VMEM((LEAF, RANK), f32),
            pltpu.VMEM((4, 2, LEAF, RANK), f32),
            pltpu.VMEM((2, RANK, LEAF), f32),
            pltpu.VMEM((2, RANK, 2 * RANK), f32),
            pltpu.VMEM((2, RANK, 2 * RANK), f32),
            pltpu.VMEM((2, RANK, RANK), f32),
            pltpu.VMEM((2, 2, RANK, RANK), f32),
            pltpu.VMEM((2, RANK // 2, 4 * RANK), f32),
            pltpu.VMEM((RANK // 2, 4 * RANK), f32),
            pltpu.VMEM((RANK, 2 * RANK), f32),
            pltpu.VMEM((leaves, 8, RANK), f32),
            pltpu.VMEM((groups, 8, RANK), f32),
            pltpu.SMEM((2, NEAR), jnp.int32),
            pltpu.SMEM((2, NEAR), jnp.int32),
            dma((7,)),
            dma((11,)),
            dma((12,)),
            dma((leaves,)),
            dma((leaves,)),
            dma((groups,)),
            dma((groups,)),
        ],
        compiler_params=pltpu.CompilerParams(
            collective_id=0, has_side_effects=True, vmem_limit_bytes=66000000
        ),
    )(
        near_tiles.reshape(2 * NEAR, LEAF, LEAF),
        diag_tiles,
        leaf_basis,
        level1_basis,
        level2_basis,
        near_index,
        near_mask,
    )
    outs = pl.pallas_call(
        write_out,
        out_shape=(*shapes, jax.ShapeDtypeStruct((1, 1), f32)),
        in_specs=[vmem] * 6,
        out_specs=[hbm] * 5 + [pl.BlockSpec(memory_space=pltpu.SMEM)],
        scratch_shapes=[dma((5,))],
        compiler_params=pltpu.CompilerParams(vmem_limit_bytes=1 << 20),
    )(*outs)
    return (*outs[:5], outs[5].reshape(()))


def solution(mesh):
    in_specs = (
        P(AXES, None, None, None),
        P(AXES, None, None),
        P(AXES, None),
        P(AXES, None),
        P(AXES, None, None),
        P(AXES, None, None),
        P(AXES, None),
    )
    out_specs = (
        P(AXES, None, None),
        P(AXES, None, None),
        P(AXES, None),
        P(AXES, None),
        P(AXES, None),
        P(),
    )
    return jax.shard_map(
        on_device, mesh=mesh, in_specs=in_specs, out_specs=out_specs, check_vma=False
    )
```

time: 77.8 us -> 53.4 us (0.69)
  Pallas kernels: 67.9 us -> 52.7 us
  local copies, waits for them, and re-layouts: 8.97 us -> 0 us
    pallas_call x1 -> x2, Pallas kernels: 67.9 us -> 52.7 us  [the longest x1 51.4 us: on_device(): pl.pallas_call(functools.partial(kernel, groups, leaves), out_shape=tuple...]
    unnamed x17 -> x0, local copies, waits for them, and re-layouts: 8.45 us -> none
where the time goes in v2:
time: 53.4 us; the launch traced here: 53.3 us
  Pallas kernels  52.7 us (99%)
  between operations  0.64 us (1%)
    pallas_call x1, Pallas kernels, on_device(): pl.pallas_call(functools.partial(kernel, groups, leaves), out_shape=tuple...  51.4 us
    pallas_call x1, Pallas kernels, on_device(): pl.pallas_call(write_out, out_shape=(*shapes, jax.ShapeDtypeStruct((1, 1)...  1.3 us

profile of v2, /device:TPU:1, one launch (start us, length us, event | category | flops | bytes accessed | tf_op | source)
XLA Modules:
  0.0 53.3 jit_solution(14284297255226881207)
XLA Ops:
  0.6 51.4 %shard_map.118 = (f32[2,128,128]{2,1,0:T(8,128)S(1)}, f32[1,128,128]{2,1,0:T(8,128)S(1)}, f32[64,128]{1,0:T(8,128)S(1)}, f32[64,128]{1,0:T(8,128)S(1)}, f32[64,512]{1,0:T(8,128)S(1)}, /*index=5*/f32[8,128]{1,0:T(8,128)S(1)}) custom-call(f32[32,256,256]{2,1,0:T(8,128)} %bitcast.2, f32[2,256,256]{2,1,0:T(8,128)} %diag.1, f32[2,256,256]{2,1,0:T(8,128)} %leaf_basis.1, ...), custom_call_target="tpu_custom_call" | custom-call | tf_op jit(solution)/shard_map/pallas_call | solution.py:497
  52.0 1.3 %shard_map.119 = (f32[2,128,128]{2,1,0:T(8,128)}, f32[1,128,128]{2,1,0:T(8,128)}, f32[64,128]{1,0:T(8,128)}, f32[64,128]{1,0:T(8,128)}, f32[64,512]{1,0:T(8,128)}, /*index=5*/f32[1,1]{1,0:T(1,128)}) custom-call(f32[2,128,128]{2,1,0:T(8,128)S(1)} %get-tuple-element.18.refs_0_, f32[1,128,128]{2,1,0:T(8,128)S(1)} %get-tuple-element.19.refs_1_, ...), custom_call_target="tpu_custom_call" | custom-call | tf_op jit(solution)/shard_map/pallas_call | solution.py:548

commit v3 on v2

--- a/solution.py
+++ b/solution.py
@@ -141,18 +141,19 @@
     A[i, :, RANK:] = (rows == cols).astype(f32)
 
 
-def finish(VE, D, i, y, basis_t):
+def lower_factor(VE, D, i):
     rows = lax.broadcasted_iota(jnp.int32, (RANK, RANK), 0)
     cols = lax.broadcasted_iota(jnp.int32, (RANK, RANK), 1)
-    d = D[i]
-    s = rsqrt(d)
-    upper = jnp.where(cols >= rows, VE[i, :, :RANK] * s, 0.0)
-    inverse = VE[i, :, RANK:] * s
+    return jnp.where(cols >= rows, VE[i, :, :RANK] * rsqrt(D[i]), 0.0).T
+
+
+def reduced(VE, D, i, y, basis_t):
+    inverse = VE[i, :, RANK:] * rsqrt(D[i])
     xh = dot3(inverse, jnp.concatenate([y[:RANK, RANK:], basis_t[:RANK]], axis=1))
     sa = jnp.concatenate([y[RANK:, RANK:], basis_t[RANK:]], axis=1) - dot3(
         xh[:, :RANK], xh, 0, 0
     )
-    return upper.T, sa[:, :RANK], sa[:, RANK:]
+    return sa[:, :RANK], sa[:, RANK:]
 
 
 def log_rows(d):
@@ -246,7 +247,7 @@
         copy.start()
 
     barrier = pltpu.get_barrier_semaphore()
-    direct = (-side, side, 3, -3, 4, -4)
+    direct = (-side, side, 4, -4)
     for delta in direct:
         pl.semaphore_signal(barrier, inc=1, device_id=device(shifted(delta)), device_id_type=MESH)
 
@@ -321,8 +322,8 @@
     schur = []
     logs = jnp.zeros((1, RANK), f32)
     for i in range(2):
-        lower, s, a_t = finish(VE, D, i, yv[i], bt[i])
-        F0[i] = lower
+        s, a_t = reduced(VE, D, i, yv[i], bt[i])
+        F0[i] = lower_factor(VE, D, i)
         at[i] = a_t
         schur.append(s)
         logs = logs + log_rows(D[i])
@@ -339,9 +340,6 @@
         slot = 4 + delta
         pltpu.make_async_copy(win.at[slot], win.at[slot], recv_sem.at[slot]).wait()
 
-    arrived(side)
-    relay_in = remote(win.at[4 + side], win.at[4 + 2 * side], 7, 4 + 2 * side, sibling)
-    relay_in.start()
     eliminate(A, VE, D, 1)
     arrived(-side)
 
@@ -352,23 +350,31 @@
             z = z + dot3n(tile, win[4 - side, c] * live)
         zsib[i * RANK : (i + 1) * RANK] = dot3(at[i], z)
 
-    lower, s, a1_t = finish(VE, D, 0, yv[0], bt[0])
-    F1[0] = lower
-    logs = logs + log_rows(D[0])
+    s, a1_t = reduced(VE, D, 0, yv[0], bt[0])
     ex[par, 0] = s
     ex[par, 1] = dot3(a1_t, zsib[...])
     ex_send = remote(ex.at[par], ex.at[par], 9, 10, sibling)
     ex_send.start()
+    F1[0] = lower_factor(VE, D, 0)
+    logs = logs + log_rows(D[0])
+    arrived(side)
+    relays = [
+        remote(win.at[4 + side], win.at[4 - 3 * side], 4, 4 - 3 * side, shifted(4 * side)),
+        remote(us, win.at[4 + 3 * side], 5, 4 + 3 * side, shifted(-4 * side)),
+        remote(us, win.at[4 - 2 * side], 8, 4 - 2 * side, shifted(side)),
+        remote(win.at[4 + side], win.at[4 + 2 * side], 7, 4 + 2 * side, sibling),
+    ]
+    relays[0].start()
 
     w_send.wait_recv()
     q2 = wv[1 - par, :, RANK:]
     for b in range(2):
         us[b] = dot3(win[4 - side, b], q2)
+    relays[1].start()
+    relays[2].start()
     zu[...] = jnp.zeros_like(zu)
     w = jnp.concatenate([wv[0], wv[1]], axis=0)
     bt[0] = w.T
-    relay_out = remote(us, win.at[4 - 2 * side], 8, 4 - 2 * side, shifted(side))
-    relay_out.start()
 
     def far(delta):
         e = (par + delta + 8) // 2 - 4
@@ -382,16 +388,19 @@
 
     far(side)
     arrived(4)
+    arrived(-4)
     far(4)
+    far(-4)
 
     ex_send.wait_recv()
+    relays[3].start()
     system = block_system(ex[0, 0], ex[0, 1], ex[1, 1], ex[1, 0])
     y = dot3(bt[0], dot3(system, w))
     yv[0] = y
     load_system(A, 0, y[:RANK, :RANK])
     eliminate(A, VE, D, 1)
     logs = logs + log_rows(D[0]) * jnp.where(par == 0, 1.0, 0.0)
-    la[l] = jnp.broadcast_to(logs, (8, RANK))
+    la[l] = logs
 
     def to_leaf(t, wait):
         copy = pltpu.make_async_remote_copy(
@@ -429,23 +438,23 @@
         lax.fori_loop(1, size, body, 0)
 
     each(leaves, to_leaf, False)
-    lower, s, a2_t = finish(VE, D, 0, yv[0], bt[0])
+    s, a2_t = reduced(VE, D, 0, yv[0], bt[0])
     half = pl.multiple_of(par * (RANK // 2), RANK // 2)
-    f2[:, :RANK] = lower
+    f2[:, :RANK] = lower_factor(VE, D, 0)
     f2[:, RANK:] = s
     F2[...] = f2[pl.ds(half, RANK // 2), :RANK]
     S2[...] = f2[pl.ds(half, RANK // 2), RANK:]
     chain = dot3(jnp.where(par == 0, a2_t[:, :RANK], a2_t[:, RANK:]), a1_t)
-    for delta in (-4, 3, -3):
+    for delta in (-3 * side, 3 * side):
         arrived(delta)
         far(delta)
     each(leaves, to_leaf, True)
     lg[g] = jnp.sum(la[...], axis=0)
     each(groups, to_group, False)
+    arrived(-2 * side)
+    far(-2 * side)
     arrived(2 * side)
     far(2 * side)
-    arrived(-2 * side)
-    far(-2 * side)
     below = jnp.concatenate(
         [
             jnp.concatenate([dot3(at[a], zu[e, a]) for e in range(4)], axis=1)
@@ -462,8 +471,8 @@
         copy.wait_send()
     w_send.wait_send()
     ex_send.wait_send()
-    relay_in.wait_send()
-    relay_out.wait_send()
+    for copy in relays:
+        copy.wait_send()
     p_send.wait()
     C2[...] = pp[par] + pr[...]
     each(groups, to_group, True)
@@ -496,7 +505,7 @@
     )
     outs = pl.pallas_call(
         functools.partial(kernel, groups, leaves),
-        out_shape=tuple(pltpu.VMEM(x.shape, f32) for x in shapes) + (pltpu.VMEM((8, RANK), f32),),
+        out_shape=tuple(pltpu.VMEM(x.shape, f32) for x in shapes) + (pltpu.VMEM((1, RANK), f32),),
         in_specs=[hbm] * 7,
         out_specs=[vmem] * 6,
         scratch_shapes=[
@@ -521,8 +530,8 @@
             pltpu.VMEM((2, RANK // 2, 4 * RANK), f32),
             pltpu.VMEM((RANK // 2, 4 * RANK), f32),
             pltpu.VMEM((RANK, 2 * RANK), f32),
-            pltpu.VMEM((leaves, 8, RANK), f32),
-            pltpu.VMEM((groups, 8, RANK), f32),
+            pltpu.VMEM((leaves, 1, RANK), f32),
+            pltpu.VMEM((groups, 1, RANK), f32),
             pltpu.SMEM((2, NEAR), jnp.int32),
             pltpu.SMEM((2, NEAR), jnp.int32),
             dma((7,)),

time: 53.4 us -> 47.5 us (0.89); the launches traced: 53.3 us -> 46.5 us
  Pallas kernels: 52.7 us -> 45.9 us
    pallas_call x1, Pallas kernels: 51.4 us -> 44.6 us  [on_device(): pl.pallas_call(functools.partial(kernel, groups, leaves), out_shape=tuple...]
where the time goes in v3:
time: 47.5 us; the launch traced here: 46.5 us
  Pallas kernels  45.9 us (97%)
  between operations  0.64 us (1%)
    pallas_call x1, Pallas kernels, on_device(): pl.pallas_call(functools.partial(kernel, groups, leaves), out_shape=tuple...  44.6 us
    pallas_call x1, Pallas kernels, on_device(): pl.pallas_call(write_out, out_shape=(*shapes, jax.ShapeDtypeStruct((1, 1)...  1.3 us

profile of v3, /device:TPU:1, one launch (start us, length us, event | category | flops | bytes accessed | tf_op | source)
XLA Modules:
  0.0 46.5 jit_solution(17328814199411650661)
XLA Ops:
  0.6 44.6 %shard_map.118 = (f32[2,128,128]{2,1,0:T(8,128)S(1)}, f32[1,128,128]{2,1,0:T(8,128)S(1)}, f32[64,128]{1,0:T(8,128)S(1)}, f32[64,128]{1,0:T(8,128)S(1)}, f32[64,512]{1,0:T(8,128)S(1)}, /*index=5*/f32[1,128]{1,0:T(1,128)S(1)}) custom-call(f32[32,256,256]{2,1,0:T(8,128)} %bitcast.2, f32[2,256,256]{2,1,0:T(8,128)} %diag.1, f32[2,256,256]{2,1,0:T(8,128)} %leaf_basis.1, ...), custom_call_target="tpu_custom_call" | custom-call | tf_op jit(solution)/shard_map/pallas_call | solution.py:506
  45.2 1.3 %shard_map.119 = (f32[2,128,128]{2,1,0:T(8,128)}, f32[1,128,128]{2,1,0:T(8,128)}, f32[64,128]{1,0:T(8,128)}, f32[64,128]{1,0:T(8,128)}, f32[64,512]{1,0:T(8,128)}, /*index=5*/f32[1,1]{1,0:T(1,128)}) custom-call(f32[2,128,128]{2,1,0:T(8,128)S(1)} %get-tuple-element.18.refs_0_, f32[1,128,128]{2,1,0:T(8,128)S(1)} %get-tuple-element.19.refs_1_, ...), custom_call_target="tpu_custom_call" | custom-call | tf_op jit(solution)/shard_map/pallas_call | solution.py:557

commit v4 on v3

--- a/solution.py
+++ b/solution.py
@@ -33,14 +33,6 @@
     return dg(ah, bh, ca, cb) + (dg(ah, bl, ca, cb) + dg(al, bh, ca, cb))
 
 
-def outer3(v, r):
-    vh, vl = split(v)
-    rh, rl = split(r)
-    left = jnp.concatenate([vh, vl], axis=0)
-    right = jnp.concatenate([rh, rh], axis=0)
-    return dg(left, right, 0, 0) + dg(vh, rl, 0, 0)
-
-
 def rowb(x, j):
     return jnp.broadcast_to(x[j : j + 1, :], x.shape)
 
@@ -54,103 +46,120 @@
     return s * (1.5 - (0.5 * d) * (s * s))
 
 
-def dot3n(a, b):
+def halves(b):
+    bh, bl = split(b)
+    return jnp.concatenate([bh, bl], axis=1)
+
+
+def dot3n(a, wide):
     ah, al = split(a)
-    bh, bl = split(b)
-    wide = dg(ah, jnp.concatenate([bh, bl], axis=1), 1, 0)
-    n = b.shape[1]
-    return wide[:, :n] + (wide[:, n:] + dg(al, bh, 1, 0))
-
-
-def pivots(state, n):
+    n = wide.shape[1] // 2
+    both = dg(ah, wide, 1, 0)
+    return both[:, :n] + (both[:, n:] + dg(al, wide[:, :n], 1, 0))
+
+
+def eliminate(A, E, D, Zh, Zl, n, base):
+    ahead = n == 1
     row = lax.broadcasted_iota(jnp.int32, (8, 128), 0)
-    one = jnp.ones((8, 128), f32)
-    full = [[x0, x1, cb, x0, x1, one, one] for x0, x1, cb in state]
-    for j in range(8):
-        for i in range(n):
-            x0, x1, cb, v0, v1, d, rr = full[i]
-            b = rowb(cb[j], j)
-            r0 = pl.reciprocal(b, approx=True)
-            e = 2.0 - b * r0
-            r = r0 * e
-            e = 2.0 - b * r
-            here = row == j
-            m = jnp.where(here, 0.0, cb[j] * r) * e
-            v0 = jnp.where(here, x0, v0)
-            v1 = jnp.where(here, x1, v1)
-            d = jnp.where(here, b, d)
-            rr = jnp.where(here, r * e, rr)
-            cb = [cb[q] - m * rowb(cb[q], j) if q > j else cb[q] for q in range(8)]
-            x0 = x0 - m * rowb(x0, j)
-            x1 = x1 - m * rowb(x1, j)
-            full[i] = [x0, x1, cb, v0, v1, d, rr]
-    return full
-
-
-def eliminate(A, VE, D, n):
-    ahead = n == 1
+    col = lax.broadcasted_iota(jnp.int32, (8, 128), 1)
 
     def body(k, carry):
         kk = pl.multiple_of(8 * k, 8)
         kn = pl.multiple_of(8 * jnp.minimum(k + 1, 15), 8)
         before = 8 * jnp.maximum(k - 1, 0)
+        now = jnp.logical_and(col >= kk, col < kk + 8)
+        last = jnp.logical_and(col >= kk - 8, col < kk)
+        last_all = jnp.broadcast_to(last[0:1, :], (RANK, RANK))
+        unit = (col == row + kk).astype(f32)
         state = []
-        rest = []
         for i in range(n):
-            c0, c1, v0, v1, rr, p0, p1 = carry[i]
-            scaled = jnp.concatenate([v0 * rr, v1 * rr], axis=1)
+            c, p = carry[i]
             if ahead:
                 nxt = A[i, pl.ds(kn, 8), :]
-                A[i] = A[i] - outer3(v0, scaled)
-            else:
-                A[i] = A[i] - outer3(v0, scaled)
+            whole = A[i]
+            hi, lo = split(whole)
+            zh, zl = Zh[i], Zl[i]
+            update = dg(hi, zh, 1, 0) + (dg(hi, zl, 1, 0) + dg(lo, zh, 1, 0))
+            A[i] = jnp.where(last_all, 0.0, whole) - update
+            if not ahead:
                 nxt = A[i, pl.ds(kn, 8), :]
-            n0, n1 = nxt[:, :128], nxt[:, 128:]
-            cb = [lane(c0, kk + j) for j in range(8)]
+            cb = [lane(c, kk + j) for j in range(8)]
             if ahead:
-                fb = [lane(n0, before + j) for j in range(8)]
+                fb = [lane(nxt, before + j) for j in range(8)]
+                nxt = jnp.where(last, 0.0, nxt)
                 for j in range(8):
-                    n0 = n0 - fb[j] * rowb(p0, j)
-                    n1 = n1 - fb[j] * rowb(p1, j)
-            nb = [lane(n0, kk + j) for j in range(8)]
-            state.append([c0, c1, cb])
-            rest.append([n0, n1, nb])
-        full = pivots(state, n)
+                    nxt = nxt - fb[j] * rowb(p, j)
+            nb = [lane(nxt, kk + j) for j in range(8)]
+            nxt = jnp.where(now, 0.0, nxt)
+            x = jnp.where(now, unit, c)
+            one = jnp.ones_like(c)
+            state.append([x, nxt, cb, nb, x, one, one])
+        for j in range(8):
+            for i in range(n):
+                x, nxt, cb, nb, v, d, rr = state[i]
+                b = rowb(cb[j], j)
+                r = pl.reciprocal(b, approx=True)
+                e = 2.0 - b * r
+                here = row == j
+                m = jnp.where(here, 0.0, cb[j] * r) * e
+                v = jnp.where(here, x, v)
+                d = jnp.where(here, b, d)
+                rr = jnp.where(here, r * e, rr)
+                cb = [cb[q] - m * rowb(cb[q], j) if q > j else cb[q] for q in range(8)]
+                x = x - m * rowb(x, j)
+                state[i] = [x, nxt, cb, nb, v, d, rr]
+        even = lax.rem(k, 2) == 0
+        pair = pl.multiple_of(16 * (k // 2), 16)
+        old = pl.multiple_of(16 * (jnp.maximum(k - 1, 0) // 2), 16)
         result = []
         for i in range(n):
-            x0, x1, _, v0, v1, d, rr = full[i]
-            n0, n1, nb = rest[i]
-            p0, p1 = x0 * rr, x1 * rr
+            x, nxt, cb, nb, v, d, rr = state[i]
+            p = x * rr
             for j in range(8):
-                n0 = n0 - nb[j] * rowb(p0, j)
-                n1 = n1 - nb[j] * rowb(p1, j)
-            VE[i, pl.ds(kk, 8), :] = jnp.concatenate([v0, v1], axis=1)
-            D[i, pl.ds(kk, 8), :] = d
-            result.append((n0, n1, v0, v1, rr, p0, p1))
+                nxt = nxt - nb[j] * rowb(p, j)
+            E[base + i, pl.ds(kk, 8), :] = v
+            D[base + i, pl.ds(kk, 8), :] = d
+            none = jnp.zeros((16, RANK), bf16)
+            Zh[i, pl.ds(old, 16), :] = none
+            Zl[i, pl.ds(old, 16), :] = none
+            hi, lo = split(
+                jnp.concatenate([jnp.where(even, p, 0.0), jnp.where(even, 0.0, p)], axis=0)
+            )
+            Zh[i, pl.ds(pair, 16), :] = hi
+            Zl[i, pl.ds(pair, 16), :] = lo
+            result.append((nxt, p))
         return tuple(result)
 
-    zero = jnp.zeros((8, 128), f32)
-    start = tuple((A[i, 0:8, :128], A[i, 0:8, 128:]) + (zero,) * 5 for i in range(n))
-    lax.fori_loop(0, 16, body, start)
-
-
-def load_system(A, i, y_rr):
+    Zh[...] = jnp.zeros_like(Zh)
+    Zl[...] = jnp.zeros_like(Zl)
+    zero = jnp.zeros((8, RANK), f32)
+    lax.fori_loop(0, 16, body, tuple((A[i, 0:8, :], zero) for i in range(n)))
+
+
+def lower_mask():
     rows = lax.broadcasted_iota(jnp.int32, (RANK, RANK), 0)
     cols = lax.broadcasted_iota(jnp.int32, (RANK, RANK), 1)
-    A[i, :, :RANK] = y_rr
-    A[i, :, RANK:] = (rows == cols).astype(f32)
-
-
-def lower_factor(VE, D, i):
-    rows = lax.broadcasted_iota(jnp.int32, (RANK, RANK), 0)
-    cols = lax.broadcasted_iota(jnp.int32, (RANK, RANK), 1)
-    return jnp.where(cols >= rows, VE[i, :, :RANK] * rsqrt(D[i]), 0.0).T
-
-
-def reduced(VE, D, i, y, basis_t):
-    inverse = VE[i, :, RANK:] * rsqrt(D[i])
-    xh = dot3(inverse, jnp.concatenate([y[:RANK, RANK:], basis_t[:RANK]], axis=1))
-    sa = jnp.concatenate([y[RANK:, RANK:], basis_t[RANK:]], axis=1) - dot3(
+    return cols <= rows
+
+
+def lower_factor(E, y, i):
+    product = lax.dot_general(
+        y[i, :RANK, :RANK],
+        E[i],
+        (((1,), (1,)), ((), ())),
+        precision=lax.Precision.HIGHEST,
+        preferred_element_type=f32,
+    )
+    return jnp.where(lower_mask(), product, 0.0)
+
+
+def reduced(E, D, y, i, basis_t):
+    inverse = jnp.where(lower_mask(), E[i] * rsqrt(D[i]), 0.0)
+    E[i] = inverse
+    xh = dot3(
+        inverse, jnp.concatenate([y[i, :RANK, RANK:], basis_t[:RANK]], axis=1)
+    )
+    sa = jnp.concatenate([y[i, RANK:, RANK:], basis_t[RANK:]], axis=1) - dot3(
         xh[:, :RANK], xh, 0, 0
     )
     return sa[:, :RANK], sa[:, RANK:]
@@ -201,8 +210,10 @@
     zu,
     at,
     A,
-    VE,
+    E,
     D,
+    Zh,
+    Zl,
     ex,
     pp,
     pr,
@@ -218,6 +229,8 @@
     la_recv,
     lg_send,
     lg_recv,
+    part_send,
+    part_recv,
 ):
     count = groups * leaves
     g = lax.axis_index("grp")
@@ -243,7 +256,7 @@
         pltpu.make_async_copy(mask_hbm, mask, load_sem.at[5]),
         pltpu.make_async_copy(near, nv, load_sem.at[6]),
     ]
-    for copy in loads[:4]:
+    for copy in loads[:3]:
         copy.start()
 
     barrier = pltpu.get_barrier_semaphore()
@@ -265,6 +278,7 @@
 
     lax.fori_loop(1, leaves, greet_leaf, 0)
     lax.fori_loop(1, groups, greet_group, 0)
+    loads[3].start()
 
     for copy in loads[:3]:
         copy.wait()
@@ -281,7 +295,8 @@
         bt[i] = bv[i].T
         y = dot3(bt[i], dot3(dv[i], bv[i]))
         yv[i] = y
-        load_system(A, i, y[:RANK, :RANK])
+        A[i] = y[:RANK, :RANK]
+    bt[2] = b1v[...].T
 
     pl.semaphore_wait(barrier, len(direct) + (leaves - 1) + (groups - 1))
 
@@ -306,7 +321,7 @@
     for copy in sends[2:]:
         copy.start()
 
-    eliminate(A, VE, D, 2)
+    eliminate(A, E, D, Zh, Zl, 2, 0)
     for copy in loads[4:]:
         copy.wait()
 
@@ -320,43 +335,39 @@
         return nv[a * NEAR + slot], live
 
     schur = []
-    logs = jnp.zeros((1, RANK), f32)
     for i in range(2):
-        s, a_t = reduced(VE, D, i, yv[i], bt[i])
-        F0[i] = lower_factor(VE, D, i)
+        s, a_t = reduced(E, D, yv, i, bt[i])
         at[i] = a_t
         schur.append(s)
-        logs = logs + log_rows(D[i])
         tile, live = near_block(i, 2 * m + 1 - i)
-        zown[i] = dot3n(tile, bv[1 - i, :, RANK:] * live)
+        zown[i] = dot3n(tile, halves(bv[1 - i, :, RANK:])) * live
 
     system = block_system(schur[0], dot3(at[0], zown[0]), dot3(at[1], zown[1]), schur[1])
-    bt[0] = b1v[...].T
-    y = dot3(bt[0], dot3(system, b1v[...]))
-    yv[0] = y
-    load_system(A, 0, y[:RANK, :RANK])
+    y = dot3(bt[2], dot3(system, b1v[...]))
+    yv[2] = y
+    A[0] = y[:RANK, :RANK]
 
     def arrived(delta):
         slot = 4 + delta
         pltpu.make_async_copy(win.at[slot], win.at[slot], recv_sem.at[slot]).wait()
 
-    eliminate(A, VE, D, 1)
+    eliminate(A, E, D, Zh, Zl, 1, 2)
     arrived(-side)
 
+    right = [halves(win[4 - side, c]) for c in range(2)]
     for i in range(2):
         z = jnp.zeros((LEAF, RANK), f32)
         for c in range(2):
             tile, live = near_block(i, 2 * sibling + c)
-            z = z + dot3n(tile, win[4 - side, c] * live)
+            z = z + dot3n(tile, right[c]) * live
         zsib[i * RANK : (i + 1) * RANK] = dot3(at[i], z)
 
-    s, a1_t = reduced(VE, D, 0, yv[0], bt[0])
+    s, a1_t = reduced(E, D, yv, 2, bt[2])
     ex[par, 0] = s
+    ex_sends = [remote(ex.at[par, i], ex.at[par, i], 9 + 2 * i, 10 + 2 * i, sibling) for i in range(2)]
+    ex_sends[0].start()
     ex[par, 1] = dot3(a1_t, zsib[...])
-    ex_send = remote(ex.at[par], ex.at[par], 9, 10, sibling)
-    ex_send.start()
-    F1[0] = lower_factor(VE, D, 0)
-    logs = logs + log_rows(D[0])
+    ex_sends[1].start()
     arrived(side)
     relays = [
         remote(win.at[4 + side], win.at[4 - 3 * side], 4, 4 - 3 * side, shifted(4 * side)),
@@ -371,19 +382,19 @@
     for b in range(2):
         us[b] = dot3(win[4 - side, b], q2)
     relays[1].start()
-    relays[2].start()
     zu[...] = jnp.zeros_like(zu)
     w = jnp.concatenate([wv[0], wv[1]], axis=0)
-    bt[0] = w.T
+    bt[3] = w.T
 
     def far(delta):
         e = (par + delta + 8) // 2 - 4
         slot_e = jnp.where(e < 0, e + 2, e + 1)
+        right = [halves(win[4 + delta, b]) for b in range(2)]
         for a in range(2):
             z = zu[slot_e, a]
             for b in range(2):
                 tile, live = near_block(a, 2 * (m + delta) + b)
-                z = z + dot3n(tile, win[4 + delta, b] * live)
+                z = z + dot3n(tile, right[b]) * live
             zu[slot_e, a] = z
 
     far(side)
@@ -392,14 +403,21 @@
     far(4)
     far(-4)
 
-    ex_send.wait_recv()
+    for i in range(2):
+        F0[i] = lower_factor(E, yv, i)
+    F1[0] = lower_factor(E, yv, 2)
+    logs = log_rows(D[0]) + log_rows(D[1]) + log_rows(D[2])
+
+    for copy in ex_sends:
+        copy.wait_recv()
+    relays[2].start()
     relays[3].start()
     system = block_system(ex[0, 0], ex[0, 1], ex[1, 1], ex[1, 0])
-    y = dot3(bt[0], dot3(system, w))
-    yv[0] = y
-    load_system(A, 0, y[:RANK, :RANK])
-    eliminate(A, VE, D, 1)
-    logs = logs + log_rows(D[0]) * jnp.where(par == 0, 1.0, 0.0)
+    y = dot3(bt[3], dot3(system, w))
+    yv[3] = y
+    A[0] = y[:RANK, :RANK]
+    eliminate(A, E, D, Zh, Zl, 1, 3)
+    logs = logs + log_rows(D[3]) * jnp.where(par == 0, 1.0, 0.0)
     la[l] = logs
 
     def to_leaf(t, wait):
@@ -438,43 +456,57 @@
         lax.fori_loop(1, size, body, 0)
 
     each(leaves, to_leaf, False)
-    s, a2_t = reduced(VE, D, 0, yv[0], bt[0])
+    s, a2_t = reduced(E, D, yv, 3, bt[3])
     half = pl.multiple_of(par * (RANK // 2), RANK // 2)
-    f2[:, :RANK] = lower_factor(VE, D, 0)
+    f2[:, :RANK] = lower_factor(E, yv, 3)
     f2[:, RANK:] = s
     F2[...] = f2[pl.ds(half, RANK // 2), :RANK]
     S2[...] = f2[pl.ds(half, RANK // 2), RANK:]
     chain = dot3(jnp.where(par == 0, a2_t[:, :RANK], a2_t[:, RANK:]), a1_t)
-    for delta in (-3 * side, 3 * side):
-        arrived(delta)
-        far(delta)
+
+    def reduce_part(e):
+        i = jnp.where(e < 0, e + 2, e + 1)
+        below = jnp.concatenate([dot3(at[a], zu[i, a]) for a in range(2)], axis=0)
+        part = dot3(chain, below)
+        pp[0, i] = part[: RANK // 2]
+        pp[1, i] = part[RANK // 2 :]
+        copy = pltpu.make_async_remote_copy(
+            src_ref=pp.at[1 - par, i],
+            dst_ref=pr.at[i],
+            send_sem=part_send.at[i],
+            recv_sem=part_recv.at[i],
+            device_id=device(sibling),
+            device_id_type=MESH,
+        )
+        copy.start()
+        return copy
+
+    parts = [reduce_part(-2 * side)]
+    arrived(-3 * side)
+    far(-3 * side)
+    arrived(-2 * side)
+    far(-2 * side)
+    parts.append(reduce_part(-side))
     each(leaves, to_leaf, True)
     lg[g] = jnp.sum(la[...], axis=0)
     each(groups, to_group, False)
-    arrived(-2 * side)
-    far(-2 * side)
+    arrived(3 * side)
+    far(3 * side)
+    parts.append(reduce_part(2 * side))
     arrived(2 * side)
     far(2 * side)
-    below = jnp.concatenate(
-        [
-            jnp.concatenate([dot3(at[a], zu[e, a]) for e in range(4)], axis=1)
-            for a in range(2)
-        ],
-        axis=0,
-    )
-    part = dot3(chain, below)
-    pp[0] = part[: RANK // 2]
-    pp[1] = part[RANK // 2 :]
-    p_send = remote(pp.at[1 - par], pr, 10, 11, sibling)
-    p_send.start()
+    parts.append(reduce_part(side))
     for copy in sends:
         copy.wait_send()
     w_send.wait_send()
-    ex_send.wait_send()
+    for copy in ex_sends:
+        copy.wait_send()
     for copy in relays:
         copy.wait_send()
-    p_send.wait()
-    C2[...] = pp[par] + pr[...]
+    for copy in parts:
+        copy.wait()
+    for i in range(4):
+        C2[:, i * RANK : (i + 1) * RANK] = pp[par, i] + pr[i]
     each(groups, to_group, True)
     LD[...] = jnp.sum(lg[...], axis=0)
 
@@ -514,8 +546,8 @@
             pltpu.VMEM((2, LEAF, LEAF), f32),
             pltpu.VMEM((LEAF, LEAF), f32),
             pltpu.VMEM((2, RANK, LEAF), f32),
-            pltpu.VMEM((2, LEAF, LEAF), f32),
-            pltpu.VMEM((2, LEAF, LEAF), f32),
+            pltpu.VMEM((4, LEAF, LEAF), f32),
+            pltpu.VMEM((4, LEAF, LEAF), f32),
             pltpu.VMEM((2, 2, LEAF, RANK), f32),
             pltpu.VMEM((2, LEAF, RANK), f32),
             pltpu.VMEM((9, 2, LEAF, RANK), f32),
@@ -523,24 +555,28 @@
             pltpu.VMEM((LEAF, RANK), f32),
             pltpu.VMEM((4, 2, LEAF, RANK), f32),
             pltpu.VMEM((2, RANK, LEAF), f32),
-            pltpu.VMEM((2, RANK, 2 * RANK), f32),
-            pltpu.VMEM((2, RANK, 2 * RANK), f32),
             pltpu.VMEM((2, RANK, RANK), f32),
+            pltpu.VMEM((4, RANK, RANK), f32),
+            pltpu.VMEM((4, RANK, RANK), f32),
+            pltpu.VMEM((2, RANK, RANK), bf16),
+            pltpu.VMEM((2, RANK, RANK), bf16),
             pltpu.VMEM((2, 2, RANK, RANK), f32),
-            pltpu.VMEM((2, RANK // 2, 4 * RANK), f32),
-            pltpu.VMEM((RANK // 2, 4 * RANK), f32),
+            pltpu.VMEM((2, 4, RANK // 2, RANK), f32),
+            pltpu.VMEM((4, RANK // 2, RANK), f32),
             pltpu.VMEM((RANK, 2 * RANK), f32),
             pltpu.VMEM((leaves, 1, RANK), f32),
             pltpu.VMEM((groups, 1, RANK), f32),
             pltpu.SMEM((2, NEAR), jnp.int32),
             pltpu.SMEM((2, NEAR), jnp.int32),
             dma((7,)),
-            dma((11,)),
             dma((12,)),
+            dma((13,)),
             dma((leaves,)),
             dma((leaves,)),
             dma((groups,)),
             dma((groups,)),
+            dma((4,)),
+            dma((4,)),
         ],
         compiler_params=pltpu.CompilerParams(
             collective_id=0, has_side_effects=True, vmem_limit_bytes=66000000

time: 47.5 us -> 44.8 us (0.943); the launches traced: 46.5 us -> 44.7 us
  Pallas kernels: 45.9 us -> 44 us
    pallas_call x1, Pallas kernels: 44.6 us -> 42.7 us  [on_device(): pl.pallas_call(functools.partial(kernel, groups, leaves), out_shape=tuple...]
where the time goes in v4:
time: 44.8 us; the launch traced here: 44.7 us
  Pallas kernels  44 us (98%)
  between operations  0.64 us (1%)
    pallas_call x1, Pallas kernels, on_device(): pl.pallas_call(functools.partial(kernel, groups, leaves), out_shape=tuple...  42.7 us
    pallas_call x1, Pallas kernels, on_device(): pl.pallas_call(write_out, out_shape=(*shapes, jax.ShapeDtypeStruct((1, 1)...  1.3 us

profile of v4, /device:TPU:1, one launch (start us, length us, event | category | flops | bytes accessed | tf_op | source)
XLA Modules:
  0.0 44.7 jit_solution(14327696280888440806)
XLA Ops:
  0.6 42.7 %shard_map.118 = (f32[2,128,128]{2,1,0:T(8,128)S(1)}, f32[1,128,128]{2,1,0:T(8,128)S(1)}, f32[64,128]{1,0:T(8,128)S(1)}, f32[64,128]{1,0:T(8,128)S(1)}, f32[64,512]{1,0:T(8,128)S(1)}, /*index=5*/f32[1,128]{1,0:T(1,128)S(1)}) custom-call(f32[32,256,256]{2,1,0:T(8,128)} %bitcast.2, f32[2,256,256]{2,1,0:T(8,128)} %diag.1, f32[2,256,256]{2,1,0:T(8,128)} %leaf_basis.1, ...), custom_call_target="tpu_custom_call" | custom-call | tf_op jit(solution)/shard_map/pallas_call | solution.py:538
  43.4 1.3 %shard_map.119 = (f32[2,128,128]{2,1,0:T(8,128)}, f32[1,128,128]{2,1,0:T(8,128)}, f32[64,128]{1,0:T(8,128)}, f32[64,128]{1,0:T(8,128)}, f32[64,512]{1,0:T(8,128)}, /*index=5*/f32[1,1]{1,0:T(1,128)}) custom-call(f32[2,128,128]{2,1,0:T(8,128)S(1)} %get-tuple-element.18.refs_0_, f32[1,128,128]{2,1,0:T(8,128)S(1)} %get-tuple-element.19.refs_1_, ...), custom_call_target="tpu_custom_call" | custom-call | tf_op jit(solution)/shard_map/pallas_call | solution.py:593

commit v5 on v4

--- a/solution.py
+++ b/solution.py
@@ -58,7 +58,7 @@
     return both[:, :n] + (both[:, n:] + dg(al, wide[:, :n], 1, 0))
 
 
-def eliminate(A, E, D, Zh, Zl, n, base):
+def eliminate(A, E, D, Zh, Zl, n, base, first=0, last=16, carry=None):
     ahead = n == 1
     row = lax.broadcasted_iota(jnp.int32, (8, 128), 0)
     col = lax.broadcasted_iota(jnp.int32, (8, 128), 1)
@@ -68,8 +68,8 @@
         kn = pl.multiple_of(8 * jnp.minimum(k + 1, 15), 8)
         before = 8 * jnp.maximum(k - 1, 0)
         now = jnp.logical_and(col >= kk, col < kk + 8)
-        last = jnp.logical_and(col >= kk - 8, col < kk)
-        last_all = jnp.broadcast_to(last[0:1, :], (RANK, RANK))
+        past = jnp.logical_and(col >= kk - 8, col < kk)
+        past_all = jnp.broadcast_to(past[0:1, :], (RANK, RANK))
         unit = (col == row + kk).astype(f32)
         state = []
         for i in range(n):
@@ -80,13 +80,13 @@
             hi, lo = split(whole)
             zh, zl = Zh[i], Zl[i]
             update = dg(hi, zh, 1, 0) + (dg(hi, zl, 1, 0) + dg(lo, zh, 1, 0))
-            A[i] = jnp.where(last_all, 0.0, whole) - update
+            A[i] = jnp.where(past_all, 0.0, whole) - update
             if not ahead:
                 nxt = A[i, pl.ds(kn, 8), :]
             cb = [lane(c, kk + j) for j in range(8)]
             if ahead:
                 fb = [lane(nxt, before + j) for j in range(8)]
-                nxt = jnp.where(last, 0.0, nxt)
+                nxt = jnp.where(past, 0.0, nxt)
                 for j in range(8):
                     nxt = nxt - fb[j] * rowb(p, j)
             nb = [lane(nxt, kk + j) for j in range(8)]
@@ -130,10 +130,12 @@
             result.append((nxt, p))
         return tuple(result)
 
-    Zh[...] = jnp.zeros_like(Zh)
-    Zl[...] = jnp.zeros_like(Zl)
-    zero = jnp.zeros((8, RANK), f32)
-    lax.fori_loop(0, 16, body, tuple((A[i, 0:8, :], zero) for i in range(n)))
+    if carry is None:
+        Zh[...] = jnp.zeros_like(Zh)
+        Zl[...] = jnp.zeros_like(Zl)
+        zero = jnp.zeros((8, RANK), f32)
+        carry = tuple((A[i, 0:8, :], zero) for i in range(n))
+    return lax.fori_loop(first, last, body, carry)
 
 
 def lower_mask():
@@ -298,6 +300,7 @@
         A[i] = y[:RANK, :RANK]
     bt[2] = b1v[...].T
 
+    carry = eliminate(A, E, D, Zh, Zl, 2, 0, 0, 4)
     pl.semaphore_wait(barrier, len(direct) + (leaves - 1) + (groups - 1))
 
     def remote(src, dst, sent, received, target):
@@ -321,7 +324,7 @@
     for copy in sends[2:]:
         copy.start()
 
-    eliminate(A, E, D, Zh, Zl, 2, 0)
+    eliminate(A, E, D, Zh, Zl, 2, 0, 4, 16, carry)
     for copy in loads[4:]:
         copy.wait()
 
@@ -352,6 +355,10 @@
         pltpu.make_async_copy(win.at[slot], win.at[slot], recv_sem.at[slot]).wait()
 
     eliminate(A, E, D, Zh, Zl, 1, 2)
+    s, a1_t = reduced(E, D, yv, 2, bt[2])
+    ex[par, 0] = s
+    ex_sends = [remote(ex.at[par, i], ex.at[par, i], 9 + 2 * i, 10 + 2 * i, sibling) for i in range(2)]
+    ex_sends[0].start()
     arrived(-side)
 
     right = [halves(win[4 - side, c]) for c in range(2)]
@@ -362,10 +369,6 @@
             z = z + dot3n(tile, right[c]) * live
         zsib[i * RANK : (i + 1) * RANK] = dot3(at[i], z)
 
-    s, a1_t = reduced(E, D, yv, 2, bt[2])
-    ex[par, 0] = s
-    ex_sends = [remote(ex.at[par, i], ex.at[par, i], 9 + 2 * i, 10 + 2 * i, sibling) for i in range(2)]
-    ex_sends[0].start()
     ex[par, 1] = dot3(a1_t, zsib[...])
     ex_sends[1].start()
     arrived(side)
@@ -382,6 +385,7 @@
     for b in range(2):
         us[b] = dot3(win[4 - side, b], q2)
     relays[1].start()
+    relays[2].start()
     zu[...] = jnp.zeros_like(zu)
     w = jnp.concatenate([wv[0], wv[1]], axis=0)
     bt[3] = w.T
@@ -398,11 +402,8 @@
             zu[slot_e, a] = z
 
     far(side)
-    arrived(4)
-    arrived(-4)
-    far(4)
-    far(-4)
-
+    arrived(-4 * side)
+    far(-4 * side)
     for i in range(2):
         F0[i] = lower_factor(E, yv, i)
     F1[0] = lower_factor(E, yv, 2)
@@ -410,7 +411,6 @@
 
     for copy in ex_sends:
         copy.wait_recv()
-    relays[2].start()
     relays[3].start()
     system = block_system(ex[0, 0], ex[0, 1], ex[1, 1], ex[1, 0])
     y = dot3(bt[3], dot3(system, w))
@@ -453,7 +453,8 @@
             step(t, wait)
             return 0
 
-        lax.fori_loop(1, size, body, 0)
+        lax.fori_loop(size // 2 - 1, size, body, 0)
+        lax.fori_loop(1, size // 2 - 1, body, 0)
 
     each(leaves, to_leaf, False)
     s, a2_t = reduced(E, D, yv, 3, bt[3])
@@ -487,6 +488,8 @@
     arrived(-2 * side)
     far(-2 * side)
     parts.append(reduce_part(-side))
+    arrived(4 * side)
+    far(4 * side)
     each(leaves, to_leaf, True)
     lg[g] = jnp.sum(la[...], axis=0)
     each(groups, to_group, False)

time: 44.8 us -> 43.8 us (0.978)
  Pallas kernels: 44 us -> 43 us
    pallas_call x1, Pallas kernels: 42.7 us -> 41.7 us  [on_device(): pl.pallas_call(functools.partial(kernel, groups, leaves), out_shape=tuple...]
where the time goes in v5:
time: 43.8 us; the launch traced here: 43.7 us
  Pallas kernels  43 us (98%)
  between operations  0.64 us (1%)
    pallas_call x1, Pallas kernels, on_device(): pl.pallas_call(functools.partial(kernel, groups, leaves), out_shape=tuple...  41.7 us
    pallas_call x1, Pallas kernels, on_device(): pl.pallas_call(write_out, out_shape=(*shapes, jax.ShapeDtypeStruct((1, 1)...  1.3 us

profile of v5, /device:TPU:1, one launch (start us, length us, event | category | flops | bytes accessed | tf_op | source)
XLA Modules:
  0.0 43.7 jit_solution(9731015052811132074)
XLA Ops:
  0.6 41.7 %shard_map.118 = (f32[2,128,128]{2,1,0:T(8,128)S(1)}, f32[1,128,128]{2,1,0:T(8,128)S(1)}, f32[64,128]{1,0:T(8,128)S(1)}, f32[64,128]{1,0:T(8,128)S(1)}, f32[64,512]{1,0:T(8,128)S(1)}, /*index=5*/f32[1,128]{1,0:T(1,128)S(1)}) custom-call(f32[32,256,256]{2,1,0:T(8,128)} %bitcast.2, f32[2,256,256]{2,1,0:T(8,128)} %diag.1, f32[2,256,256]{2,1,0:T(8,128)} %leaf_basis.1, ...), custom_call_target="tpu_custom_call" | custom-call | tf_op jit(solution)/shard_map/pallas_call | solution.py:541
  42.4 1.3 %shard_map.119 = (f32[2,128,128]{2,1,0:T(8,128)}, f32[1,128,128]{2,1,0:T(8,128)}, f32[64,128]{1,0:T(8,128)}, f32[64,128]{1,0:T(8,128)}, f32[64,512]{1,0:T(8,128)}, /*index=5*/f32[1,1]{1,0:T(1,128)}) custom-call(f32[2,128,128]{2,1,0:T(8,128)S(1)} %get-tuple-element.18.refs_0_, f32[1,128,128]{2,1,0:T(8,128)S(1)} %get-tuple-element.19.refs_1_, ...), custom_call_target="tpu_custom_call" | custom-call | tf_op jit(solution)/shard_map/pallas_call | solution.py:596
